TPU v7x, 512 devices: a whole 4x4x16 slice. The times are simulated.
512 devices in a mesh: seq: 32 (over z, core), cp: 16 (over x, y).
Axes of the slice: x: 4, y: 4, z: 16, core: 2. Of those that a mesh axis runs over, the one named last changes fastest.
Arguments:
- queries: bfloat16 [65536, 768], P(('seq', 'cp')), parts along dimension 0, may hold values from -6 to 6, as said below
- keys: bfloat16 [65536, 128], P(('seq', 'cp')), parts along dimension 0, may hold values from -6 to 6, as said below
- values: bfloat16 [65536, 128], P(('seq', 'cp')), parts along dimension 0, may hold values from -6 to 6
- out_grad: bfloat16 [65536, 768], P(('seq', 'cp')), parts along dimension 0, may hold values from -6 to 6
- positions: int32 [3, 65536], P(None, 'seq'), parts along dimension 1, may hold values from 0 to 2047
- doc_ids: int32 [65536], P('seq'), parts along dimension 0, may hold values from 0 to 7, never falling along the last dimension, each value on 1 to 1024 neighbouring positions
- stretch_order: int32 [1024], P('seq'), parts along dimension 0, may hold values from 0 to 31, each once
Outputs:
- attn_out: bfloat16 [65536, 768], P(('seq', 'cp')), parts along dimension 0
- grad_queries: bfloat16 [65536, 768], P(('seq', 'cp')), parts along dimension 0
- grad_keys: bfloat16 [65536, 128], P(('seq', 'cp')), parts along dimension 0
- grad_values: bfloat16 [65536, 128], P(('seq', 'cp')), parts along dimension 0
There are 32 independent parts, one for each index of `seq`. A program takes and returns all parts, laid end to end along the dimension named above; each array names one. Nothing has to cross between parts.
Inputs may be any that keep to these rules, and one draw needn't show every extreme that they name: `queries`: values of one part; a few tokens may have large entries. `keys`: values of one part; a few tokens may have large entries. `doc_ids`: never falls along the sequence; each document holds at most 1024 tokens. `stretch_order`: each block number appears once.
All inputs are finite; a program needn't handle non-finite values.
Results may differ from a plain program's by a relative error of at most 0.01.
Values may be sent and summed in bfloat16 or wider, within the bound.
No kernel may reach another device: no remote copies, remote signals or barrier semaphores. Data moves between devices by JAX's collectives and lax.ppermute only.
A program may use at most 64 MiB of HBM per device.

v0:
```python
import math

import jax
import jax.numpy as jnp
from jax import lax
from jax.sharding import PartitionSpec as P

HQ = 6
HK = 1
HD = 128
SEC_T = 16
SEC_H = 24


def sent_to_all(array, axis):
    copies = jnp.broadcast_to(array, (lax.axis_size(axis), *array.shape))
    return lax.all_to_all(copies, axis, split_axis=0, concat_axis=0, tiled=True)


def in_order(blocks, dim):
    blocks = jnp.moveaxis(blocks, 0, dim)
    lengths = blocks.shape
    return blocks.reshape(*lengths[:dim], lengths[dim] * lengths[dim + 1], *lengths[dim + 2 :])


def gathered_copies(array, axis, dim):
    blocks = sent_to_all(array, axis)
    return in_order(blocks, dim)


def in_one_piece(arrays, axis, dim, along):
    ends, at = ([], 0)
    for a in arrays[:-1]:
        at += a.shape[along]
        ends.append(at)
    both = jnp.concatenate(arrays, axis=along)
    return tuple(jnp.split(gathered_copies(both, axis, dim), ends, axis=along))


def cut_along(array, dim, count):
    lengths = array.shape
    blocks = array.reshape(*lengths[:dim], count, lengths[dim] // count, *lengths[dim + 1 :])
    return jnp.moveaxis(blocks, dim, 0)


def sent_and_summed(array, axis, dim):
    count = lax.axis_size(axis)
    blocks = lax.all_to_all(cut_along(array, dim, count), axis, 0, 0, tiled=True)
    return jnp.sum(blocks, axis=0)


def rotary_tables(pos3):
    half = HD // 2
    pairs = jnp.arange(half, dtype=jnp.int32)
    freqs = jnp.exp(-(2.0 * pairs.astype(jnp.float32) / HD) * math.log(1000000.0))
    pos_f = pos3.astype(jnp.float32)
    chosen = jnp.where(
        (pairs < SEC_T)[None, :],
        pos_f[0][:, None],
        jnp.where((pairs < SEC_T + SEC_H)[None, :], pos_f[1][:, None], pos_f[2][:, None]),
    )
    angle = chosen * freqs[None, :]
    cosine = jnp.concatenate([jnp.cos(angle), jnp.cos(angle)], axis=1)
    sine_tab = jnp.concatenate([jnp.sin(angle), jnp.sin(angle)], axis=1)
    return (cosine, sine_tab)


def rotate(field, cosine, sine_tab):
    half = HD // 2
    first, second = (field[..., :half], field[..., half:])
    turned = jnp.concatenate([-second, first], axis=-1)
    return field * cosine[:, None, :] + turned * sine_tab[:, None, :]


def rotate_back(field, cosine, sine_tab):
    half = HD // 2
    scaled = field * sine_tab[:, None, :]
    turned = jnp.concatenate([scaled[..., half:], -scaled[..., :half]], axis=-1)
    return field * cosine[:, None, :] + turned


def dot_nt(left, right):
    return lax.dot_general(
        left, right, (((1,), (1,)), ((), ())), preferred_element_type=jnp.float32
    )


def dot_tn(left, right):
    return lax.dot_general(
        left, right, (((0,), (0,)), ((), ())), preferred_element_type=jnp.float32
    )


def score_products(left, right):
    return dot_nt(left, right)


def weighted_rows(weights, right):
    return jnp.dot(weights, right, preferred_element_type=jnp.float32)


def shards(queries, keys, values, out_grad, positions, doc_ids, stretch_order):
    devices = lax.axis_size("cp")
    my_rank = lax.axis_index("cp")
    tok_rows = queries.shape[0]
    half_len = tok_rows // 2
    total = tok_rows * devices
    group_size = HQ // HK
    score_scale = 1.0 / math.sqrt(HD)
    within = jnp.arange(half_len, dtype=jnp.int32)
    order_all = (stretch_order[:, None] * half_len + within[None, :]).reshape(total)
    orig_local = lax.dynamic_slice_in_dim(order_all, my_rank * tok_rows, tok_rows)
    doc_all = doc_ids[order_all]
    doc_local = doc_ids[orig_local]
    cosine, sine_tab = rotary_tables(positions[:, orig_local])
    q_rot = rotate(queries.astype(jnp.float32).reshape(tok_rows, HQ, HD), cosine, sine_tab).astype(
        jnp.bfloat16
    )
    k_rot = rotate(keys.astype(jnp.float32).reshape(tok_rows, HK, HD), cosine, sine_tab).astype(
        jnp.bfloat16
    )
    k_flat = k_rot.reshape(tok_rows, HK * HD)
    keys_all, values_all = in_one_piece((k_flat, values), "cp", 0, 1)
    allowed = (doc_local[:, None] == doc_all[None, :]) & (order_all[None, :] <= orig_local[:, None])
    mask_rows = jnp.repeat(allowed, group_size, axis=0)
    grad_heads = out_grad.reshape(tok_rows, HQ, HD)
    outputs, dq_list, dscore_list, prob_list, query_list, dout_list, lse_list, delta_list = (
        [],
        [],
        [],
        [],
        [],
        [],
        [],
        [],
    )
    q_grp = q_rot.reshape(tok_rows * group_size, HD)
    do_grp = grad_heads.reshape(tok_rows * group_size, HD)
    scores = score_products(q_grp, keys_all) * score_scale
    scores = jnp.where(mask_rows, scores, -jnp.inf)
    top = jnp.max(scores, axis=-1, keepdims=True)
    expo = jnp.exp(scores - top)
    row_total = jnp.sum(expo, axis=-1, keepdims=True)
    probs32 = expo / row_total
    probs = probs32.astype(jnp.bfloat16)
    outputs.append(weighted_rows(probs, values_all).astype(jnp.bfloat16))
    dprobs = score_products(do_grp, values_all)
    delta = jnp.sum(probs32 * dprobs, axis=-1, keepdims=True)
    dscores = (probs32 * (dprobs - delta)).astype(jnp.bfloat16)
    dq_list.append(
        (weighted_rows(dscores, keys_all) * score_scale).reshape(tok_rows, group_size, HD)
    )
    dscore_list.append(dscores)
    prob_list.append(probs)
    query_list.append(q_grp)
    dout_list.append(do_grp)
    lse_list.append((top + jnp.log(row_total)).reshape(tok_rows, group_size))
    delta_list.append(delta.reshape(tok_rows, group_size))
    attn_out = (
        jnp.stack(outputs, axis=0)
        .reshape(HK, tok_rows, group_size * HD)
        .transpose(1, 0, 2)
        .reshape(tok_rows, HQ * HD)
    )
    dq_rot = dq_list[0]
    pieces = []
    group_id = 0
    part_ds = dscore_list[group_id]
    pieces.append(dot_tn(part_ds, query_list[group_id]) * score_scale)
    group_id = 0
    part_pr = prob_list[group_id]
    pieces.append(dot_tn(part_pr, dout_list[group_id]))
    summed = sent_and_summed(jnp.concatenate(pieces, axis=1), "cp", 0)
    dk_rot = summed[:, : HK * HD].reshape(tok_rows, HK, HD)
    grad_values = summed[:, HK * HD :].astype(jnp.bfloat16)
    grad_queries = (
        rotate_back(dq_rot, cosine, sine_tab).astype(jnp.bfloat16).reshape(tok_rows, HQ * HD)
    )
    grad_keys = (
        rotate_back(dk_rot, cosine, sine_tab).astype(jnp.bfloat16).reshape(tok_rows, HK * HD)
    )
    return (attn_out, grad_queries, grad_keys, grad_values)


def solution(mesh):
    placed = (
        P(("seq", "cp"), None),
        P(("seq", "cp"), None),
        P(("seq", "cp"), None),
        P(("seq", "cp"), None),
        P(None, "seq"),
        P("seq"),
        P("seq"),
    )
    return jax.shard_map(
        shards,
        mesh=mesh,
        in_specs=placed,
        out_specs=(
            P(("seq", "cp"), None),
            P(("seq", "cp"), None),
            P(("seq", "cp"), None),
            P(("seq", "cp"), None),
        ),
        check_vma=False,
    )
```

profile of v0, /device:TPU:480, one launch (start us, length us, event | category | flops | bytes accessed | tf_op | source)
XLA Modules:
  0.0 90.9 jit_solution(7268043772104459240)
XLA Ops:
  0.7 0.7 broadcast_multiply_fusion.1
  1.6 0.9 copy.31
  2.4 0.9 copy.32
  3.3 1.1 %copy.26 = s32[3,2048]{0,1:T(8,128)S(1)} copy(s32[3,2048]{1,0:T(4,128)} %param.11) | data formatting | bytes 49152 | tf_op args[4]
  4.5 0.6 gather_fusion.2
  6.3 1.1 %broadcast_in_dim.90 = bf16[16,128,256]{2,1,0:T(8,128)(2,1)} broadcast(bf16[128,256]{1,0:T(8,128)(2,1)S(1)} %copy.33), dimensions={1,2} | broadcast | bytes 1114112 | tf_op jit(solution)/shard_map/broadcast_in_dim | solution.py:16
  7.4 7.2 %all-to-all-start = ((bf16[16,128,256]{2,1,0:T(8,128)(2,1)}), bf16[16,128,256]{2,1,0:T(8,128)(2,1)S(1)}, u32[]{:S(2)}, u32[]{:S(2)}) async-start(bf16[16,128,256]{2,1,0:T(8,128)(2,1)} %broadcast_in_dim.90), calls=%async_computation | async-start | bytes 2097152 | tf_op jit(solution)/shard_map/all_to_all | solution.py:17
  14.7 1.1 %copy.24 = bf16[128,768]{0,1:T(8,128)(2,1)S(1)} copy(bf16[128,768]{1,0:T(8,128)(2,1)} %param.7) | data formatting | bytes 393216 | tf_op args[0]
  16.0 1.1 %gather_fusion = s32[128]{0:T(128)S(1)} fusion(s32[2048]{0:T(1024)S(1)} %copy-done, s32[1024]{0:T(1024)S(1)} %pad_clamp_fusion), kind=kCustom, calls=%fused_computation | custom fusion | bytes 1536 | tf_op jit(solution)/shard_map/gather | solution.py:114
  17.2 11.8 %gather_fusion.1 = s32[2048]{0:T(1024)S(1)} fusion(s32[2048]{0:T(1024)S(1)} %copy-done, s32[2048]{0:T(1024)S(1)} %broadcast_clamp_fusion), kind=kCustom, calls=%fused_computation.1 | custom fusion | bytes 24576 | tf_op jit(solution)/shard_map/gather | solution.py:113
  29.2 0.8 reshape.131
  30.2 0.8 concatenate.42
  31.3 0.8 concatenate.43
  32.3 0.8 mul.118
  33.1 0.8 mul.121
  34.2 1.2 %broadcast_in_dim.81 = pred[128,6,2048]{2,1,0:T(8,128)(4,1)S(1)} broadcast(pred[128,2048]{1,0:T(8,128)(4,1)S(1)} %compare_and_fusion), dimensions={0,2} | broadcast | bytes 1835008 | tf_op jit(solution)/shard_map/broadcast_in_dim | solution.py:125
  35.5 2.5 %reshape.130 = pred[768,2048]{1,0:T(32,128)(4,1)} reshape(pred[128,6,2048]{2,1,0:T(8,128)(4,1)S(1)} %broadcast_in_dim.81) | data formatting | bytes 3145728 | tf_op jit(solution)/shard_map/reshape | solution.py:125
  38.0 1.6 %fusion.18 = bf16[768,128]{1,0:T(8,128)(2,1)S(1)} fusion(f32[768,128]{1,0:T(8,128)} %mul.121, f32[768,64]{1,0:T(8,128)} %concatenate.43, f32[768,64]{1,0:T(8,128)} %concatenate.42, f32[768,128]{1,0:T(8,128)} %reshape.131, f32[768,128]{1,0:T(8,128)} %mul.118), kind=kLoop, calls=%fused_computation.31 | loop fusion | flops 491520 | bytes 1769472 | tf_op jit(solution)/shard_map/convert_element_type | solution.py:116
  39.6 3.1 %fusion.29 = (f32[768]{0:T(1024)S(1)}, f32[768,2048]{1,0:T(8,128)S(1)}) fusion(pred[768,2048]{1,0:T(32,128)(4,1)} %reshape.130, bf16[768,128]{1,0:T(8,128)(2,1)S(1)} %fusion.18, bf16[2048,256]{1,0:T(8,128)(2,1)S(1)} %bitcast.45), kind=kOutput, calls=%fused_computation.72 | convolution fusion | flops 407371008 | bytes 8588288 | tf_op jit(solution)/shard_map/dot_general | solution.py:83
  42.8 1.0 %fusion.4 = f32[768]{0:T(1024)S(1)} fusion(f32[768,2048]{1,0:T(8,128)S(1)} %get-tuple-element.33, f32[768]{0:T(1024)S(1)} %get-tuple-element.32), kind=kLoop, calls=%fused_computation.11 | loop fusion | flops 3144960 | bytes 6297600 | tf_op jit(solution)/shard_map/reduce_sum | solution.py:143
  43.8 1.8 %fusion = (f32[768]{0:T(1024)S(1)}, f32[768,2048]{1,0:T(8,128)S(1)}, f32[2048,768]{0,1:T(8,128)S(1)}) fusion(f32[768]{0:T(1024)S(1)} %fusion.4, f32[768,2048]{1,0:T(8,128)S(1)} %get-tuple-element.33, f32[768]{0:T(1024)S(1)} %get-tuple-element.32, bf16[768,128]{1,0:T(8,128)(2,1)S(1)} %reshape_reshape.3, bf16[2048,256]{1,0:T(8,128)(2,1)S(1)} %bitcast.46), kind=kOutput, calls=%fused_computation.5 | convolution fusion | flops 408943872 | bytes 19606528 | tf_op jit(solution)/shard_map/dot_general | solution.py:83
  46.2 2.0 %copy-done.1 = f32[768,2048]{1,0:T(8,128)} copy-done((f32[768,2048]{1,0:T(8,128)}, f32[768,2048]{1,0:T(8,128)S(1)}, u32[]{:S(2)}) %copy-start.1) | copy-done | bytes 6291480
  49.5 1.6 %copy_bitcast_fusion = f32[16,128,256]{1,2,0:T(8,128)} fusion(f32[2048,128]{0,1:T(8,128)S(1)} %fusion.5, f32[2048,128]{0,1:T(8,128)S(1)} %convolution_multiply_fusion), kind=kLoop, calls=%fused_computation.13 | loop fusion | flops 524288 | bytes 4194304 | tf_op jit(solution)/shard_map/reshape | solution.py:42
  51.1 7.3 %all-to-all-start.1 = ((f32[16,128,256]{1,2,0:T(8,128)}), f32[16,128,256]{1,2,0:T(8,128)}, u32[]{:S(2)}, u32[]{:S(2)}) async-start(f32[16,128,256]{1,2,0:T(8,128)} %copy_bitcast_fusion), calls=%async_computation.1 | async-start | bytes 4194304 | tf_op jit(solution)/shard_map/all_to_all | solution.py:48
  58.4 2.0 %convolution_multiply_fusion.1 = f32[768,128]{1,0:T(8,128)S(1)} fusion(bf16[768,2048]{1,0:T(8,128)(2,1)S(1)} %fusion.2, bf16[2048,256]{1,0:T(8,128)(2,1)} %bitcast.47), kind=kOutput, calls=%fused_computation.19 | convolution fusion | flops 402751488 | bytes 4063232 | tf_op jit(solution)/shard_map/dot_general | solution.py:99
  60.5 3.9 %fusion.9 = bf16[768,128]{1,0:T(8,128)(2,1)S(1)} fusion(f32[768,2048]{1,0:T(8,128)} %copy-done.1, bf16[2048,256]{1,0:T(8,128)(2,1)} %bitcast.48), kind=kOutput, calls=%fused_computation.20 | convolution fusion | flops 404324352 | bytes 7012352 | tf_op jit(solution)/shard_map/dot_general | solution.py:99
  64.4 0.9 reshape_transpose_reshape_stack.3
  66.2 0.8 copy.39
  67.0 20.6 %all-to-all-done.1 = f32[16,128,256]{1,2,0:T(8,128)} async-done(((f32[16,128,256]{1,2,0:T(8,128)}), f32[16,128,256]{1,2,0:T(8,128)}, u32[]{:S(2)}, u32[]{:S(2)}) %all-to-all-start.1) | async-done | bytes 2097184 | tf_op jit(solution)/shard_map/all_to_all | solution.py:48
  87.7 1.7 %reduce_sum.29 = f32[128,256]{0,1:T(8,128)S(1)} reduce(f32[16,128,256]{1,2,0:T(8,128)} %all-to-all-done.1, f32[]{:T(128)} %constant.6.clone.1), dimensions={0}, to_apply=%region_3.4 | reduce | flops 491520 | bytes 2228228 | tf_op jit(solution)/shard_map/reduce_sum | solution.py:49
  89.4 0.7 copy.41
  90.2 0.7 copy.40
  (67 shorter events, 5.9 us)
Async XLA Ops:
  0.6 15.4 %copy-start = (s32[2048]{0:T(1024)S(1)}, s32[2048]{0:T(1024)}, u32[]{:S(2)}) copy-start(s32[2048]{0:T(1024)} %param.12) | copy-start | bytes 24580
  5.6 0.6 copy-start.7
  5.6 23.4 %copy-start.9 = (f32[128,64]{0,1:T(8,128)}, f32[128,64]{0,1:T(8,128)S(1)}, u32[]{:S(2)}) copy-start(f32[128,64]{0,1:T(8,128)S(1)} %get-tuple-element.30) | copy-start | bytes 98308
  6.2 26.0 %copy-start.3 = (f32[128,128]{0,1:T(8,128)}, f32[128,128]{0,1:T(8,128)S(1)}, u32[]{:S(2)}) copy-start(f32[128,128]{0,1:T(8,128)S(1)} %get-tuple-element.27) | copy-start | bytes 196612
  7.4 21.5 %copy-start.11 = (bf16[128,768]{1,0:T(8,128)(2,1)S(1)}, bf16[128,768]{1,0:T(8,128)(2,1)}, u32[]{:S(2)}) copy-start(bf16[128,768]{1,0:T(8,128)(2,1)} %param.10) | copy-start | bytes 589828
  7.4 32.2 %all-to-all-start = ((bf16[16,128,256]{2,1,0:T(8,128)(2,1)}), bf16[16,128,256]{2,1,0:T(8,128)(2,1)S(1)}, u32[]{:S(2)}, u32[]{:S(2)}) async-start(bf16[16,128,256]{2,1,0:T(8,128)(2,1)} %broadcast_in_dim.90), calls=%async_computation | async-start | bytes 2097152 | tf_op jit(solution)/shard_map/all_to_all | solution.py:17
  32.1 3.3 %copy-start.5 = (f32[128,128]{1,0:T(8,128)}, f32[128,128]{1,0:T(8,128)S(1)}, u32[]{:S(2)}) copy-start(f32[128,128]{1,0:T(8,128)S(1)} %copy.30) | copy-start | bytes 196612
  39.6 4.1 %copy-start.2 = (bf16[16,128,256]{2,1,0:T(8,128)(2,1)}, bf16[16,128,256]{2,1,0:T(8,128)(2,1)S(1)}, u32[]{:S(2)}) copy-start(bf16[16,128,256]{2,1,0:T(8,128)(2,1)S(1)} %all-to-all-done) | copy-start | bytes 3145732
  45.6 2.7 %copy-start.1 = (f32[768,2048]{1,0:T(8,128)}, f32[768,2048]{1,0:T(8,128)S(1)}, u32[]{:S(2)}) copy-start(f32[768,2048]{1,0:T(8,128)S(1)} %get-tuple-element.16) | copy-start | bytes 18874372
  51.1 36.6 %all-to-all-start.1 = ((f32[16,128,256]{1,2,0:T(8,128)}), f32[16,128,256]{1,2,0:T(8,128)}, u32[]{:S(2)}, u32[]{:S(2)}) async-start(f32[16,128,256]{1,2,0:T(8,128)} %copy_bitcast_fusion), calls=%async_computation.1 | async-start | bytes 4194304 | tf_op jit(solution)/shard_map/all_to_all | solution.py:48
  60.4 5.1 %copy-start.6 = (f32[128,128]{1,0:T(8,128)S(1)}, f32[128,128]{1,0:T(8,128)}, u32[]{:S(2)}) copy-start(f32[128,128]{1,0:T(8,128)} %copy-done.5) | copy-start | bytes 196612
  60.5 5.6 %copy-start.4 = (f32[128,128]{0,1:T(8,128)S(1)}, f32[128,128]{0,1:T(8,128)}, u32[]{:S(2)}) copy-start(f32[128,128]{0,1:T(8,128)} %copy-done.3) | copy-start | bytes 196612
  64.4 25.0 %copy-start.8 = (f32[128,64]{0,1:T(8,128)S(1)}, f32[128,64]{0,1:T(8,128)}, u32[]{:S(2)}) copy-start(f32[128,64]{0,1:T(8,128)} %copy-done.7) | copy-start | bytes 98308
  64.4 25.7 %copy-start.10 = (f32[128,64]{0,1:T(8,128)S(1)}, f32[128,64]{0,1:T(8,128)}, u32[]{:S(2)}) copy-start(f32[128,64]{0,1:T(8,128)} %copy-done.9) | copy-start | bytes 98308
where the time goes:
time: 91.6 us; the launch traced here: 90.9 us
  local copies, waits for them, and re-layouts  34.1 us (37%)
  waiting for transfers between devices  20.6 us (22%)
  starting transfers between devices  14.4 us (16%)
  matrix products  12.1 us (13%)
  other arithmetic  8.51 us (9%)
  between operations  1.15 us (1%)
    all_to_all x1, waiting for transfers between devices, sent_and_summed(): lax.all_to_all(cut_along(array, dim, count), axis, 0, 0, tiled=True)  20.6 us
    gather x1, local copies, waits for them, and re-layouts, shards(): doc_all = doc_ids[order_all]  11.8 us
    unnamed x32, local copies, waits for them, and re-layouts  8.97 us
    all_to_all x1, starting transfers between devices, sent_and_summed(): lax.all_to_all(cut_along(array, dim, count), axis, 0, 0, tiled=True)  7.28 us
    all_to_all x1, starting transfers between devices, sent_to_all(): return lax.all_to_all(copies, axis, split_axis=0, concat_axis=0, tiled=True)  7.17 us
    dot_general x2, matrix products, weighted_rows(): return jnp.dot(weights, right, preferred_element_type=jnp.float32)  5.88 us
    dot_general x2, matrix products, dot_nt(): lax.dot_general(left, right, (((1,), (1,)), ((), ())), preferred_element_...  4.94 us
    reshape x1, local copies, waits for them, and re-layouts, shards(): mask_rows = jnp.repeat(allowed, group_size, axis=0)  2.5 us
  transfers between devices with their start and end apart: 2, of which 1 were waited for; matrix products, arithmetic and copies ran while one was open for 37% of the time, Pallas kernels for 0%

commit v1 on v0

v1 whole, which is shorter than its diff:
```python
import functools
import math

import jax
import jax.numpy as jnp
from jax import lax
from jax.experimental import pallas as pl
from jax.experimental.pallas import tpu as pltpu
from jax.sharding import PartitionSpec as P

HQ = 6
HD = 128
HALF = HD // 2
SEC_T = 16
SEC_H = 24
STRETCH = 64
DOCS = 8
CHUNK = 256
SUB = 32
LANES = HQ * STRETCH
SCALE = 1.0 / math.sqrt(HD)
LOG2E = math.log2(math.e)

F32 = jnp.float32
BF16 = jnp.bfloat16


def dot_nt(left, right):
    return lax.dot_general(left, right, (((1,), (1,)), ((), ())), preferred_element_type=F32)


def dot_tn(left, right):
    return lax.dot_general(left, right, (((0,), (0,)), ((), ())), preferred_element_type=F32)


def dot_nn(left, right):
    return lax.dot_general(left, right, (((1,), (0,)), ((), ())), preferred_element_type=F32)


def rotated(x, cosine, signed_sine):
    return x * cosine + pltpu.roll(x, HALF, 1) * signed_sine


def rotated_back(x, cosine, signed_sine):
    return x * cosine - pltpu.roll(x, HALF, 1) * signed_sine


def keys_kernel(order_ref, keys_ref, values_ref, pos_ref, payload_ref, cos_ref, sin_ref):
    me = lax.axis_index("cp")
    rows = keys_ref.shape[0]
    lane = lax.broadcasted_iota(jnp.int32, (1, rows), 1)
    windows = []
    for place in range(2):
        stretch = order_ref[2 * me + place]
        start = pl.multiple_of((stretch // 2) * 128, 128)
        window = pos_ref[:, pl.ds(start, 128)].astype(F32)
        turned = pltpu.roll(window, HALF, 1)
        windows.append(jnp.where(stretch % 2 == place, window, turned))
    pos = jnp.where(lane < STRETCH, windows[0], windows[1])
    pair = lax.broadcasted_iota(jnp.int32, (HALF, 1), 0)
    freq = jnp.exp(-(2.0 * pair.astype(F32) / HD) * math.log(1000000.0))
    chosen = jnp.where(
        pair < SEC_T, pos[0:1, :], jnp.where(pair < SEC_T + SEC_H, pos[1:2, :], pos[2:3, :])
    )
    angle = chosen * freq
    table = jnp.concatenate([jnp.cos(angle), jnp.sin(angle)], axis=0).T
    other = pltpu.roll(table, HALF, 1)
    column = lax.broadcasted_iota(jnp.int32, (1, HD), 1)
    cosine = jnp.where(column < HALF, table, other)
    signed_sine = jnp.where(column < HALF, -other, table)
    cos_ref[...] = cosine
    sin_ref[...] = signed_sine
    k_rot = rotated(keys_ref[...].astype(F32), cosine, signed_sine).astype(BF16)
    values = values_ref[...]
    for peer in range(payload_ref.shape[0]):
        payload_ref[peer, :, :HD] = k_rot
        payload_ref[peer, :, HD:] = values


def queries_kernel(queries_ref, grad_ref, cos_ref, sin_ref, docs_ref, q_ref, do_ref, starts_ref):
    for place in range(2):
        rows = pl.ds(place * STRETCH, STRETCH)
        cosine, signed_sine = cos_ref[rows, :], sin_ref[rows, :]
        for head in range(HQ):
            cols = pl.ds(head * HD, HD)
            to = pl.ds(place * LANES + head * STRETCH, STRETCH)
            q_ref[to, :] = rotated(
                queries_ref[rows, cols].astype(F32), cosine, signed_sine
            ).astype(BF16)
            do_ref[to, :] = grad_ref[rows, cols]
    docs = docs_ref[...]
    for doc in range(DOCS):
        starts_ref[doc] = jnp.sum((docs < doc).astype(jnp.int32))


def attention_kernel(
    starts_ref, order_ref, kv_ref, q_ref, do_ref, part_ref, out_ref, dq_ref,
    k_seq, v_seq, s_buf, dp_buf, dk_acc, dv_acc,
):
    me = lax.axis_index("cp")
    blocks = k_seq.shape[0] // STRETCH
    for block in range(blocks):
        to = pl.ds(pl.multiple_of(order_ref[block] * STRETCH, STRETCH), STRETCH)
        rows = pl.ds((block % 2) * STRETCH, STRETCH)
        k_seq[to, :] = kv_ref[block // 2, rows, :HD]
        v_seq[to, :] = kv_ref[block // 2, rows, HD:]
    dk_acc[...] = jnp.zeros_like(dk_acc)
    dv_acc[...] = jnp.zeros_like(dv_acc)
    tiles = LANES // 128
    lane = lax.broadcasted_iota(jnp.int32, (1, 128), 1)
    down = lax.broadcasted_iota(jnp.int32, (SUB, 128), 0)

    def one_stretch(place, carry):
        first = order_ref[2 * me + place] * STRETCH
        token = first + lane % STRETCH
        low = jnp.zeros_like(token)
        lowest = 0
        for doc in range(DOCS):
            start = starts_ref[doc]
            low = jnp.where(start <= token, jnp.maximum(low, start), low)
            lowest = jnp.where(start <= first, jnp.maximum(lowest, start), lowest)
        c_low = lowest // CHUNK
        c_high = first // CHUNK + 1
        mine = pl.ds(pl.multiple_of(place * LANES, LANES), LANES)

        def folded(x, how):
            return how(x.reshape(SUB // 8, 8, 128), axis=0)

        def scores(c, tops):
            at = pl.multiple_of(c * CHUNK, CHUNK)
            s = dot_nt(k_seq[pl.ds(at, CHUNK), :], q_ref[mine, :])
            tops = list(tops)
            for r in range(0, CHUNK, SUB):
                key = down + (at + r)
                allowed = (key >= low) & (key <= token)
                for j in range(tiles):
                    x = jnp.where(allowed, s[r : r + SUB, j * 128 : (j + 1) * 128], -jnp.inf)
                    s_buf[pl.ds(at + r, SUB), j * 128 : (j + 1) * 128] = x
                    tops[j] = jnp.maximum(tops[j], folded(x, jnp.max))
            return tuple(tops)

        tops = lax.fori_loop(
            c_low, c_high, scores, tuple(jnp.full((8, 128), -jnp.inf, F32) for _ in range(tiles))
        )
        factor = SCALE * LOG2E
        tops = [jnp.max(t, axis=0, keepdims=True) * factor for t in tops]

        def weights(c, sums):
            at = pl.multiple_of(c * CHUNK, CHUNK)
            dp = dot_nt(v_seq[pl.ds(at, CHUNK), :], do_ref[mine, :])
            totals, deltas = list(sums[0]), list(sums[1])
            for r in range(0, CHUNK, SUB):
                for j in range(tiles):
                    here = (pl.ds(at + r, SUB), slice(j * 128, (j + 1) * 128))
                    e = jnp.exp2(s_buf[here] * factor - tops[j])
                    d = dp[r : r + SUB, j * 128 : (j + 1) * 128]
                    s_buf[here] = e
                    dp_buf[here] = d
                    totals[j] = totals[j] + folded(e, jnp.sum)
                    deltas[j] = deltas[j] + folded(e * d, jnp.sum)
            return tuple(totals), tuple(deltas)

        zeros = tuple(jnp.zeros((8, 128), F32) for _ in range(tiles))
        totals, deltas = lax.fori_loop(c_low, c_high, weights, (zeros, zeros))
        inverse = [1.0 / jnp.sum(t, axis=0, keepdims=True) for t in totals]
        deltas = [jnp.sum(d, axis=0, keepdims=True) * i for d, i in zip(deltas, inverse)]
        out_ref[place] = jnp.zeros((HD, LANES), F32)
        dq_ref[place] = jnp.zeros((HD, LANES), F32)

        def gradients(c, carry):
            at = pl.multiple_of(c * CHUNK, CHUNK)
            rows = pl.ds(at, CHUNK)
            p_cols, ds_cols = [], []
            for j in range(tiles):
                p_rows, ds_rows = [], []
                for r in range(0, CHUNK, SUB):
                    here = (pl.ds(at + r, SUB), slice(j * 128, (j + 1) * 128))
                    p = s_buf[here] * inverse[j]
                    p_rows.append(p.astype(BF16))
                    ds_rows.append((p * (dp_buf[here] - deltas[j])).astype(BF16))
                p_cols.append(jnp.concatenate(p_rows, axis=0))
                ds_cols.append(jnp.concatenate(ds_rows, axis=0))
            p = jnp.concatenate(p_cols, axis=1)
            ds = jnp.concatenate(ds_cols, axis=1)
            dv_acc[rows, :] += dot_nn(p, do_ref[mine, :])
            dk_acc[rows, :] += dot_nn(ds, q_ref[mine, :])
            out_ref[place] += dot_tn(v_seq[rows, :], p)
            dq_ref[place] += dot_tn(k_seq[rows, :], ds)
            return carry

        lax.fori_loop(c_low, c_high, gradients, 0)
        return carry

    lax.fori_loop(0, 2, one_stretch, 0)
    for block in range(blocks):
        at = pl.ds(pl.multiple_of(order_ref[block] * STRETCH, STRETCH), STRETCH)
        rows = pl.ds((block % 2) * STRETCH, STRETCH)
        part_ref[block // 2, rows, :HD] = (dk_acc[at, :] * SCALE).astype(BF16)
        part_ref[block // 2, rows, HD:] = dv_acc[at, :].astype(BF16)


def outputs_kernel(out_t_ref, dq_t_ref, cos_ref, sin_ref, out_ref, dq_ref):
    for place in range(2):
        rows = pl.ds(place * STRETCH, STRETCH)
        cosine, signed_sine = cos_ref[rows, :], sin_ref[rows, :]
        out = out_t_ref[place].T
        dq = dq_t_ref[place].T
        for head in range(HQ):
            cols = pl.ds(head * HD, HD)
            part = slice(head * STRETCH, (head + 1) * STRETCH)
            out_ref[rows, cols] = out[part].astype(BF16)
            dq_ref[rows, cols] = rotated_back(dq[part] * SCALE, cosine, signed_sine).astype(BF16)


def sums_kernel(parts_ref, cos_ref, sin_ref, dk_ref, dv_ref):
    total = parts_ref[0].astype(F32)
    for peer in range(1, parts_ref.shape[0]):
        total = total + parts_ref[peer].astype(F32)
    dk_ref[...] = rotated_back(total[:, :HD], cos_ref[...], sin_ref[...]).astype(BF16)
    dv_ref[...] = total[:, HD:].astype(BF16)


VMEM = pl.BlockSpec(memory_space=pltpu.VMEM)
SMEM = pl.BlockSpec(memory_space=pltpu.SMEM)


def shards(queries, keys, values, out_grad, positions, doc_ids, stretch_order):
    devices = lax.axis_size("cp")
    rows = queries.shape[0]
    total = rows * devices
    shape = jax.ShapeDtypeStruct
    payload, cosine, signed_sine = pl.pallas_call(
        keys_kernel,
        out_shape=(
            shape((devices, rows, 2 * HD), BF16),
            shape((rows, HD), F32),
            shape((rows, HD), F32),
        ),
        in_specs=[SMEM, VMEM, VMEM, VMEM],
        out_specs=(VMEM, VMEM, VMEM),
        name="keys",
    )(stretch_order, keys, values, positions)
    q_rows, do_rows, starts = pl.pallas_call(
        queries_kernel,
        out_shape=(
            shape((rows * HQ, HD), BF16),
            shape((rows * HQ, HD), BF16),
            shape((DOCS,), jnp.int32),
        ),
        in_specs=[VMEM] * 5,
        out_specs=(VMEM, VMEM, SMEM),
        name="queries",
        cost_estimate=pl.CostEstimate(flops=10**6, transcendentals=0, bytes_accessed=10**6),
    )(queries, out_grad, cosine, signed_sine, doc_ids.reshape(total // 128, 128))
    kv = lax.all_to_all(payload, "cp", 0, 0, tiled=True)
    part, out_t, dq_t = pl.pallas_call(
        attention_kernel,
        out_shape=(
            shape((devices, rows, 2 * HD), BF16),
            shape((2, HD, LANES), F32),
            shape((2, HD, LANES), F32),
        ),
        in_specs=[SMEM, SMEM, VMEM, VMEM, VMEM],
        out_specs=(VMEM, VMEM, VMEM),
        scratch_shapes=[
            pltpu.VMEM((total, HD), BF16),
            pltpu.VMEM((total, HD), BF16),
            pltpu.VMEM((total, LANES), F32),
            pltpu.VMEM((total, LANES), F32),
            pltpu.VMEM((total, HD), F32),
            pltpu.VMEM((total, HD), F32),
        ],
        name="attention",
    )(starts, stretch_order, kv, q_rows, do_rows)
    parts = lax.all_to_all(part, "cp", 0, 0, tiled=True)
    attn_out, grad_queries = pl.pallas_call(
        outputs_kernel,
        out_shape=(shape((rows, HQ * HD), BF16), shape((rows, HQ * HD), BF16)),
        in_specs=[VMEM] * 4,
        out_specs=(VMEM, VMEM),
        name="outputs",
        cost_estimate=pl.CostEstimate(flops=10**6, transcendentals=0, bytes_accessed=10**6),
    )(out_t, dq_t, cosine, signed_sine)
    grad_keys, grad_values = pl.pallas_call(
        sums_kernel,
        out_shape=(shape((rows, HD), BF16), shape((rows, HD), BF16)),
        in_specs=[VMEM] * 3,
        out_specs=(VMEM, VMEM),
        name="sums",
    )(parts, cosine, signed_sine)
    return attn_out, grad_queries, grad_keys, grad_values


def solution(mesh):
    split = P(("seq", "cp"), None)
    return jax.shard_map(
        shards,
        mesh=mesh,
        in_specs=(split, split, split, split, P(None, "seq"), P("seq"), P("seq")),
        out_specs=(split, split, split, split),
        check_vma=False,
    )
```

time: 91.6 us -> 62.7 us (0.68)
  the two profiles are of different devices: /device:TPU:480 before, /device:TPU:256 now
where the time goes in v1:
time: 62.7 us; the launch traced here: 62.2 us
  waiting for transfers between devices  31.8 us (51%)
  Pallas kernels  14.9 us (24%)
  starting transfers between devices  12.9 us (21%)
  local copies, waits for them, and re-layouts  1.95 us (3%)
  between operations  0.66 us (1%)
    all_to_all x1, waiting for transfers between devices, shards(): parts = lax.all_to_all(part, 'cp', 0, 0, tiled=True)  16 us
    all_to_all x1, waiting for transfers between devices, shards(): kv = lax.all_to_all(payload, 'cp', 0, 0, tiled=True)  15.7 us
    all_to_all x1, starting transfers between devices, shards(): kv = lax.all_to_all(payload, 'cp', 0, 0, tiled=True)  7.04 us
    pallas_call x1, Pallas kernels, shards(): pl.pallas_call(attention_kernel, out_shape=(shape((devices, rows, 2 * HD)...  6.5 us
    all_to_all x1, starting transfers between devices, shards(): parts = lax.all_to_all(part, 'cp', 0, 0, tiled=True)  5.88 us
    pallas_call x1, Pallas kernels, shards(): pl.pallas_call(keys_kernel, out_shape=(shape((devices, rows, 2 * HD), BF1...  2.26 us
    pallas_call x1, Pallas kernels, shards(): pl.pallas_call(outputs_kernel, out_shape=(shape((rows, HQ * HD), BF16), s...  2.14 us
    pallas_call x1, Pallas kernels, shards(): pl.pallas_call(sums_kernel, out_shape=(shape((rows, HD), BF16), shape((ro...  2.09 us
  transfers between devices with their start and end apart: 2, of which 2 were waited for; matrix products, arithmetic and copies ran while one was open for 0% of the time, Pallas kernels for 7%

profile of v1, /device:TPU:256, one launch (start us, length us, event | category | flops | bytes accessed | tf_op | source)
XLA Modules:
  0.0 62.2 jit_solution(6153792230240439648)
XLA Ops:
  0.6 2.3 %keys.1 = (bf16[16,128,256]{2,1,0:T(8,128)(2,1)}, f32[128,128]{1,0:T(8,128)}, f32[128,128]{1,0:T(8,128)}) custom-call(s32[32]{0:T(128)} %order_ref.3, bf16[128,128]{1,0:T(8,128)(2,1)} %keys_ref.1, bf16[128,128]{1,0:T(8,128)(2,1)} %values_ref.1, s32[3,2048]{1,0:T(4,128)} %pos_ref.1), custom_call_target="tpu_custom_call" | custom-call | tf_op jit(solution)/shard_map/keys/pallas_call | solution.py:232
  2.9 7.0 %all-to-all-start = ((bf16[16,128,256]{2,1,0:T(8,128)(2,1)}), bf16[16,128,256]{2,1,0:T(8,128)(2,1)S(1)}, u32[]{:S(2)}, u32[]{:S(2)}) async-start(bf16[16,128,256]{2,1,0:T(8,128)(2,1)} %get-tuple-element.20), calls=%async_computation | async-start | bytes 2097152 | tf_op jit(solution)/shard_map/all_to_all | solution.py:255
  9.9 1.9 %queries.1 = (bf16[768,128]{1,0:T(8,128)(2,1)}, bf16[768,128]{1,0:T(8,128)(2,1)}, s32[8]{0:T(128)}) custom-call(bf16[128,768]{1,0:T(8,128)(2,1)} %queries_ref.1, bf16[128,768]{1,0:T(8,128)(2,1)} %grad_ref.1, f32[128,128]{1,0:T(8,128)} %get-tuple-element.17.cos_ref, f32[128,128]{1,0:T(8,128)} %get-tuple-element.18.sin_ref, s32[16,128]{1,0:T(8,128)} %bitcast.1), custom_call_target="tpu_custom_call" | custom-call | flops 1000000 | bytes 1000000 | tf_op jit(solution)/shard_map/queries/pallas_call | solution.py:243
  11.9 15.7 %all-to-all-done.kv_ref = bf16[16,128,256]{2,1,0:T(8,128)(2,1)S(1)} async-done(((bf16[16,128,256]{2,1,0:T(8,128)(2,1)}), bf16[16,128,256]{2,1,0:T(8,128)(2,1)S(1)}, u32[]{:S(2)}, u32[]{:S(2)}) %all-to-all-start) | async-done | bytes 1048608 | tf_op jit(solution)/shard_map/all_to_all | solution.py:255
  27.6 0.0 copy-start.1
  27.6 1.0 %copy-done.1 = bf16[16,128,256]{2,1,0:T(8,128)(2,1)} copy-done((bf16[16,128,256]{2,1,0:T(8,128)(2,1)}, bf16[16,128,256]{2,1,0:T(8,128)(2,1)S(1)}, u32[]{:S(2)}) %copy-start.1) | copy-done | bytes 1048600
  28.6 6.5 %attention.1 = (bf16[16,128,256]{2,1,0:T(8,128)(2,1)}, f32[2,128,384]{2,1,0:T(8,128)}, f32[2,128,384]{2,1,0:T(8,128)}) custom-call(s32[8]{0:T(128)} %get-tuple-element.19.starts_ref, s32[32]{0:T(128)} %order_ref.3, bf16[16,128,256]{2,1,0:T(8,128)(2,1)} %copy-done.1, bf16[768,128]{1,0:T(8,128)(2,1)} %get-tuple-element.21.q_ref, ...), custom_call_target="tpu_custom_call" | custom-call | tf_op jit(solution)/shard_map/attention/pallas_call | solution.py:256
  35.1 5.9 %all-to-all-start.1 = ((bf16[16,128,256]{2,1,0:T(8,128)(2,1)}), bf16[16,128,256]{2,1,0:T(8,128)(2,1)S(1)}, u32[]{:S(2)}, u32[]{:S(2)}) async-start(bf16[16,128,256]{2,1,0:T(8,128)(2,1)} %get-tuple-element.27), calls=%async_computation.1 | async-start | bytes 2097152 | tf_op jit(solution)/shard_map/all_to_all | solution.py:275
  41.0 2.1 %outputs.1 = (bf16[128,768]{1,0:T(8,128)(2,1)}, bf16[128,768]{1,0:T(8,128)(2,1)}) custom-call(f32[2,128,384]{2,1,0:T(8,128)} %get-tuple-element.23.out_t_ref, f32[2,128,384]{2,1,0:T(8,128)} %get-tuple-element.24.dq_t_ref, f32[128,128]{1,0:T(8,128)} %get-tuple-element.17.cos_ref, f32[128,128]{1,0:T(8,128)} %get-tuple-element.18.sin_ref), custom_call_target="tpu_custom_call" | custom-call | flops 1000000 | bytes 1000000 | tf_op jit(solution)/shard_map/outputs/pallas_call | solution.py:276
  43.1 16.0 %all-to-all-done.1.parts_ref = bf16[16,128,256]{2,1,0:T(8,128)(2,1)S(1)} async-done(((bf16[16,128,256]{2,1,0:T(8,128)(2,1)}), bf16[16,128,256]{2,1,0:T(8,128)(2,1)S(1)}, u32[]{:S(2)}, u32[]{:S(2)}) %all-to-all-start.1) | async-done | bytes 1048608 | tf_op jit(solution)/shard_map/all_to_all | solution.py:275
  59.2 0.0 copy-start
  59.2 1.0 %copy-done = bf16[16,128,256]{2,1,0:T(8,128)(2,1)} copy-done((bf16[16,128,256]{2,1,0:T(8,128)(2,1)}, bf16[16,128,256]{2,1,0:T(8,128)(2,1)S(1)}, u32[]{:S(2)}) %copy-start) | copy-done | bytes 1048600
  60.1 2.1 %sums.1 = (bf16[128,128]{1,0:T(8,128)(2,1)}, bf16[128,128]{1,0:T(8,128)(2,1)}) custom-call(bf16[16,128,256]{2,1,0:T(8,128)(2,1)} %copy-done, f32[128,128]{1,0:T(8,128)} %get-tuple-element.17.cos_ref, f32[128,128]{1,0:T(8,128)} %get-tuple-element.18.sin_ref), custom_call_target="tpu_custom_call" | custom-call | tf_op jit(solution)/shard_map/sums/pallas_call | solution.py:284
Async XLA Ops:
  2.9 24.7 %all-to-all-start = ((bf16[16,128,256]{2,1,0:T(8,128)(2,1)}), bf16[16,128,256]{2,1,0:T(8,128)(2,1)S(1)}, u32[]{:S(2)}, u32[]{:S(2)}) async-start(bf16[16,128,256]{2,1,0:T(8,128)(2,1)} %get-tuple-element.20), calls=%async_computation | async-start | bytes 2097152 | tf_op jit(solution)/shard_map/all_to_all | solution.py:255
  27.6 1.0 %copy-start.1 = (bf16[16,128,256]{2,1,0:T(8,128)(2,1)}, bf16[16,128,256]{2,1,0:T(8,128)(2,1)S(1)}, u32[]{:S(2)}) copy-start(bf16[16,128,256]{2,1,0:T(8,128)(2,1)S(1)} %all-to-all-done.kv_ref) | copy-start | bytes 3145732
  35.1 24.1 %all-to-all-start.1 = ((bf16[16,128,256]{2,1,0:T(8,128)(2,1)}), bf16[16,128,256]{2,1,0:T(8,128)(2,1)S(1)}, u32[]{:S(2)}, u32[]{:S(2)}) async-start(bf16[16,128,256]{2,1,0:T(8,128)(2,1)} %get-tuple-element.27), calls=%async_computation.1 | async-start | bytes 2097152 | tf_op jit(solution)/shard_map/all_to_all | solution.py:275
  59.2 1.0 %copy-start = (bf16[16,128,256]{2,1,0:T(8,128)(2,1)}, bf16[16,128,256]{2,1,0:T(8,128)(2,1)S(1)}, u32[]{:S(2)}) copy-start(bf16[16,128,256]{2,1,0:T(8,128)(2,1)S(1)} %all-to-all-done.1.parts_ref) | copy-start | bytes 3145732

commit v2 on v1

v2 whole, which is shorter than its diff:
```python
import math

import jax
import jax.numpy as jnp
from jax import lax
from jax.experimental import pallas as pl
from jax.experimental.pallas import tpu as pltpu
from jax.sharding import PartitionSpec as P

HQ = 6
HD = 128
HALF = HD // 2
SEC_T = 16
SEC_H = 24
STRETCH = 64
DOCS = 8
WINDOW = 1024 + STRETCH
SUB = 32
LANES = HQ * STRETCH
SCALE = 1.0 / math.sqrt(HD)
LOG2E = math.log2(math.e)

F32 = jnp.float32
BF16 = jnp.bfloat16


def dot_nt(left, right):
    return lax.dot_general(left, right, (((1,), (1,)), ((), ())), preferred_element_type=F32)


def dot_tn(left, right):
    return lax.dot_general(left, right, (((0,), (0,)), ((), ())), preferred_element_type=F32)


def dot_nn(left, right):
    return lax.dot_general(left, right, (((1,), (0,)), ((), ())), preferred_element_type=F32)


def rotated(x, cosine, signed_sine):
    return x * cosine + pltpu.roll(x, HALF, 1) * signed_sine


def rotated_back(x, cosine, signed_sine):
    return x * cosine - pltpu.roll(x, HALF, 1) * signed_sine


def expanded(table):
    column = lax.broadcasted_iota(jnp.int32, (1, HD), 1)
    other = pltpu.roll(table, HALF, 1)
    return jnp.where(column < HALF, table, other), jnp.where(column < HALF, -other, table)


def tables_kernel(
    order_ref, pos_ref, docs_ref, queries_ref, grad_ref,
    table_ref, mine_ref, q_ref, do_ref, q_t_ref, do_t_ref, starts_ref,
):
    me = lax.axis_index("cp")
    pair = lax.broadcasted_iota(jnp.int32, (HALF, 1), 0)
    freq = jnp.exp(-(2.0 * pair.astype(F32) / HD) * math.log(1000000.0))

    def some_tokens(c, carry):
        at = pl.ds(pl.multiple_of(c * 128, 128), 128)
        pos = pos_ref[:, at].astype(F32)
        chosen = jnp.where(
            pair < SEC_T, pos[0:1, :], jnp.where(pair < SEC_T + SEC_H, pos[1:2, :], pos[2:3, :])
        )
        angle = chosen * freq
        table_ref[at, :] = jnp.concatenate([jnp.cos(angle), jnp.sin(angle)], axis=0).T
        return carry

    lax.fori_loop(0, pos_ref.shape[1] // 128, some_tokens, 0)
    for place in range(2):
        rows = pl.ds(place * STRETCH, STRETCH)
        first = pl.multiple_of(order_ref[2 * me + place] * STRETCH, STRETCH)
        table = table_ref[pl.ds(first, STRETCH), :]
        mine_ref[rows, :] = table
        cosine, signed_sine = expanded(table)
        for head in range(HQ):
            cols = pl.ds(head * HD, HD)
            to = pl.ds(place * LANES + head * STRETCH, STRETCH)
            q_ref[to, :] = rotated(
                queries_ref[rows, cols].astype(F32), cosine, signed_sine
            ).astype(BF16)
            do_ref[to, :] = grad_ref[rows, cols]
        half = pl.ds(place * LANES, LANES)
        q_t_ref[place] = q_ref[half, :].T
        do_t_ref[place] = do_ref[half, :].T
    docs = docs_ref[...]
    for doc in range(DOCS):
        starts_ref[doc] = jnp.sum((docs < doc).astype(jnp.int32))


def attention_kernel(
    starts_ref, order_ref, kv_ref, table_ref, mine_ref, q_ref, do_ref, q_t_ref, do_t_ref,
    part_ref, out_ref, dq_ref,
    k_seq, v_seq, e_buf, dp_buf, dk_acc, dv_acc, out_buf, dq_buf, sems,
):
    me = lax.axis_index("cp")
    blocks = k_seq.shape[0] // STRETCH
    for block in range(blocks):
        to = pl.ds(pl.multiple_of(order_ref[block] * STRETCH, STRETCH), STRETCH)
        rows = pl.ds((block % 2) * STRETCH, STRETCH)
        k_seq[to, :] = rotated(
            kv_ref[block // 2, rows, :HD].astype(F32), *expanded(table_ref[to, :])
        ).astype(BF16)
        v_seq[to, :] = kv_ref[block // 2, rows, HD:]
    dk_acc[...] = jnp.zeros_like(dk_acc)
    dv_acc[...] = jnp.zeros_like(dv_acc)
    tiles = [slice(j * 128, (j + 1) * 128) for j in range(LANES // 128)]
    steps = range(0, WINDOW, SUB)
    lane = lax.broadcasted_iota(jnp.int32, (1, 128), 1)
    down = lax.broadcasted_iota(jnp.int32, (SUB, 128), 0)
    factor = SCALE * LOG2E

    def folded(x, how):
        return how(x.reshape(SUB // 8, 8, 128), axis=0)

    def one_stretch(place, carry):
        first = order_ref[2 * me + place] * STRETCH
        token = first + lane % STRETCH
        low = jnp.zeros_like(token)
        for doc in range(DOCS):
            start = starts_ref[doc]
            low = jnp.where(start <= token, jnp.maximum(low, start), low)
        base = pl.multiple_of(jnp.maximum(first + STRETCH - WINDOW, 0), STRETCH)
        window = pl.ds(base, WINDOW)
        mine = pl.ds(pl.multiple_of(place * LANES, LANES), LANES)

        s = dot_nn(k_seq[window, :], q_t_ref[place])
        tops = [jnp.full((8, 128), -jnp.inf, F32) for _ in tiles]
        for r in steps:
            key = down + (base + r)
            allowed = (key >= low) & (key <= token)
            for j, cols in enumerate(tiles):
                x = jnp.where(allowed, s[r : r + SUB, cols], -jnp.inf)
                e_buf[r : r + SUB, cols] = x
                tops[j] = jnp.maximum(tops[j], folded(x, jnp.max))
        tops = [jnp.max(t, axis=0, keepdims=True) * factor for t in tops]

        dp = dot_nn(v_seq[window, :], do_t_ref[place])
        totals = [jnp.zeros((8, 128), F32) for _ in tiles]
        deltas = [jnp.zeros((8, 128), F32) for _ in tiles]
        for r in steps:
            for j, cols in enumerate(tiles):
                e = jnp.exp2(e_buf[r : r + SUB, cols] * factor - tops[j])
                d = dp[r : r + SUB, cols]
                e_buf[r : r + SUB, cols] = e
                dp_buf[r : r + SUB, cols] = d
                totals[j] = totals[j] + folded(e, jnp.sum)
                deltas[j] = deltas[j] + folded(e * d, jnp.sum)
        inverse = [1.0 / jnp.sum(t, axis=0, keepdims=True) for t in totals]
        deltas = [jnp.sum(d, axis=0, keepdims=True) * i for d, i in zip(deltas, inverse)]

        p_cols, ds_cols = [], []
        for j, cols in enumerate(tiles):
            p_rows, ds_rows = [], []
            for r in steps:
                p = e_buf[r : r + SUB, cols] * inverse[j]
                p_rows.append(p.astype(BF16))
                ds_rows.append((p * (dp_buf[r : r + SUB, cols] - deltas[j])).astype(BF16))
            p_cols.append(jnp.concatenate(p_rows, axis=0))
            ds_cols.append(jnp.concatenate(ds_rows, axis=0))
        p = jnp.concatenate(p_cols, axis=1)
        ds = jnp.concatenate(ds_cols, axis=1)
        dv_acc[window, :] += dot_nn(p, do_ref[mine, :])
        dk_acc[window, :] += dot_nn(ds, q_ref[mine, :])
        out = dot_tn(v_seq[window, :], p).T
        dq = dot_tn(k_seq[window, :], ds).T * SCALE
        rows = pl.ds(pl.multiple_of(place * STRETCH, STRETCH), STRETCH)
        cosine, signed_sine = expanded(mine_ref[rows, :])
        for head in range(HQ):
            cols = slice(head * HD, (head + 1) * HD)
            part = slice(head * STRETCH, (head + 1) * STRETCH)
            out_buf[rows, cols] = out[part].astype(BF16)
            dq_buf[rows, cols] = rotated_back(dq[part], cosine, signed_sine).astype(BF16)
        for copy in results(place):
            copy.start()
        return carry

    def results(place):
        rows = pl.ds(pl.multiple_of(place * STRETCH, STRETCH), STRETCH)
        return (
            pltpu.make_async_copy(out_buf.at[rows], out_ref.at[rows], sems.at[0, place]),
            pltpu.make_async_copy(dq_buf.at[rows], dq_ref.at[rows], sems.at[1, place]),
        )

    lax.fori_loop(0, 2, one_stretch, 0)
    for block in range(blocks):
        at = pl.ds(pl.multiple_of(order_ref[block] * STRETCH, STRETCH), STRETCH)
        rows = pl.ds((block % 2) * STRETCH, STRETCH)
        part_ref[block // 2, rows, :HD] = (dk_acc[at, :] * SCALE).astype(BF16)
        part_ref[block // 2, rows, HD:] = dv_acc[at, :].astype(BF16)
    for place in range(2):
        for copy in results(place):
            copy.wait()


def sums_kernel(parts_ref, mine_ref, dk_ref, dv_ref):
    total = parts_ref[0].astype(F32)
    for peer in range(1, parts_ref.shape[0]):
        total = total + parts_ref[peer].astype(F32)
    dk_ref[...] = rotated_back(total[:, :HD], *expanded(mine_ref[...])).astype(BF16)
    dv_ref[...] = total[:, HD:].astype(BF16)


def params(mib):
    return pltpu.CompilerParams(vmem_limit_bytes=mib * 2**20)


VMEM = pl.BlockSpec(memory_space=pltpu.VMEM)
HBM = pl.BlockSpec(memory_space=pltpu.HBM)
SMEM = pl.BlockSpec(memory_space=pltpu.SMEM)


def shards(queries, keys, values, out_grad, positions, doc_ids, stretch_order):
    devices = lax.axis_size("cp")
    rows = queries.shape[0]
    total = rows * devices
    shape = jax.ShapeDtypeStruct
    both = jnp.concatenate([keys, values], axis=1)
    payload = jnp.broadcast_to(both, (devices, *both.shape))
    kv = lax.all_to_all(payload, "cp", 0, 0, tiled=True)
    table, mine, q_rows, do_rows, q_cols, do_cols, starts = pl.pallas_call(
        tables_kernel,
        out_shape=(
            shape((total, HD), F32),
            shape((rows, HD), F32),
            shape((2 * LANES, HD), BF16),
            shape((2 * LANES, HD), BF16),
            shape((2, HD, LANES), BF16),
            shape((2, HD, LANES), BF16),
            shape((DOCS,), jnp.int32),
        ),
        in_specs=[SMEM, VMEM, VMEM, VMEM, VMEM],
        out_specs=(VMEM,) * 6 + (SMEM,),
        compiler_params=params(16),
        name="tables",
        cost_estimate=pl.CostEstimate(flops=10**7, transcendentals=0, bytes_accessed=4 * 10**6),
    )(stretch_order, positions, doc_ids.reshape(total // 128, 128), queries, out_grad)
    part, attn_out, grad_queries = pl.pallas_call(
        attention_kernel,
        out_shape=(
            shape((devices, rows, 2 * HD), BF16),
            shape((rows, HQ * HD), BF16),
            shape((rows, HQ * HD), BF16),
        ),
        in_specs=[SMEM, SMEM] + [VMEM] * 7,
        out_specs=(VMEM, HBM, HBM),
        scratch_shapes=[
            pltpu.VMEM((total, HD), BF16),
            pltpu.VMEM((total, HD), BF16),
            pltpu.VMEM((WINDOW, LANES), F32),
            pltpu.VMEM((WINDOW, LANES), F32),
            pltpu.VMEM((total, HD), F32),
            pltpu.VMEM((total, HD), F32),
            pltpu.VMEM((rows, HQ * HD), BF16),
            pltpu.VMEM((rows, HQ * HD), BF16),
            pltpu.SemaphoreType.DMA((2, 2)),
        ],
        compiler_params=params(24),
        name="attention",
    )(starts, stretch_order, kv, table, mine, q_rows, do_rows, q_cols, do_cols)
    parts = lax.all_to_all(part, "cp", 0, 0, tiled=True)
    grad_keys, grad_values = pl.pallas_call(
        sums_kernel,
        out_shape=(shape((rows, HD), BF16), shape((rows, HD), BF16)),
        in_specs=[VMEM] * 2,
        out_specs=(VMEM, VMEM),
        compiler_params=params(16),
        name="sums",
    )(parts, mine)
    return attn_out, grad_queries, grad_keys, grad_values


def solution(mesh):
    split = P(("seq", "cp"), None)
    return jax.shard_map(
        shards,
        mesh=mesh,
        in_specs=(split, split, split, split, P(None, "seq"), P("seq"), P("seq")),
        out_specs=(split, split, split, split),
        check_vma=False,
    )
```

time: 62.7 us -> 53.2 us (0.85)
  the two profiles are of different devices: /device:TPU:256 before, /device:TPU:480 now
where the time goes in v2:
time: 53.2 us; the launch traced here: 52.9 us
  blocking collectives  18.7 us (35%)
  waiting for transfers between devices  12.2 us (23%)
  Pallas kernels  11.7 us (22%)
  starting transfers between devices  7.18 us (13%)
  local copies, waits for them, and re-layouts  1.69 us (3%)
  other arithmetic  0.78 us (1%)
  between operations  0.7 us (1%)
    all_to_all x1, blocking collectives, shards(): parts = lax.all_to_all(part, 'cp', 0, 0, tiled=True)  18.7 us
    all_to_all x1, waiting for transfers between devices, shards(): kv = lax.all_to_all(payload, 'cp', 0, 0, tiled=True)  12.2 us
    all_to_all x1, starting transfers between devices, shards(): kv = lax.all_to_all(payload, 'cp', 0, 0, tiled=True)  7.18 us
    pallas_call x1, Pallas kernels, shards(): pl.pallas_call(attention_kernel, out_shape=(shape((devices, rows, 2 * HD)...  6.04 us
    pallas_call x1, Pallas kernels, shards(): pl.pallas_call(tables_kernel, out_shape=(shape((total, HD), F32), shape((...  4.82 us
  transfers between devices with their start and end apart: 1, of which 1 were waited for; matrix products, arithmetic and copies ran while one was open for 0% of the time, Pallas kernels for 9%

profile of v2, /device:TPU:480, one launch (start us, length us, event | category | flops | bytes accessed | tf_op | source)
XLA Modules:
  0.0 52.9 jit_solution(7431025600746248467)
XLA Ops:
  0.6 0.8 %pad_maximum_fusion = bf16[128,256]{1,0:T(8,128)(2,1)S(1)} fusion(bf16[128,128]{1,0:T(8,128)(2,1)} %param.9, bf16[128,128]{1,0:T(8,128)(2,1)} %param.8), kind=kLoop, calls=%fused_computation | loop fusion | flops 131072 | bytes 131072 | tf_op jit(solution)/shard_map/concatenate | solution.py:220
  1.4 1.1 %broadcast_in_dim.3 = bf16[16,128,256]{2,1,0:T(8,128)(2,1)} broadcast(bf16[128,256]{1,0:T(8,128)(2,1)S(1)} %pad_maximum_fusion), dimensions={1,2} | broadcast | bytes 1114112 | tf_op jit(solution)/shard_map/broadcast_in_dim | solution.py:221
  2.5 0.0 copy-start
  2.5 0.0 copy-start.1
  2.5 0.0 copy-start.2
  2.5 0.0 copy-start.3
  2.5 7.2 %all-to-all-start = ((bf16[16,128,256]{2,1,0:T(8,128)(2,1)}), bf16[16,128,256]{2,1,0:T(8,128)(2,1)S(1)}, u32[]{:S(2)}, u32[]{:S(2)}) async-start(bf16[16,128,256]{2,1,0:T(8,128)(2,1)} %broadcast_in_dim.3), calls=%async_computation | async-start | bytes 2097152 | tf_op jit(solution)/shard_map/all_to_all | solution.py:222
  9.7 0.0 copy-start.4
  9.7 0.0 copy-done
  9.7 0.0 copy-done.1
  9.7 0.0 copy-done.2
  9.7 0.0 copy-done.3
  9.7 0.6 %copy-done.4 = s32[32]{0:T(128)S(1)} copy-done((s32[32]{0:T(128)S(1)}, s32[32]{0:T(128)}, u32[]{:S(2)}) %copy-start.4) | copy-done | bytes 152
  10.3 4.8 %tables.1 = (f32[2048,128]{1,0:T(8,128)S(1)}, f32[128,128]{1,0:T(8,128)S(1)}, bf16[768,128]{1,0:T(8,128)(2,1)S(1)}, bf16[768,128]{1,0:T(8,128)(2,1)S(1)}, bf16[2...) custom-call(s32[32]{0:T(128)S(1)} %copy-done.4, s32[3,2048]{1,0:T(4,128)S(1)} %copy-done.2, ...), custom_call_target="tpu_custom_call" | custom-call | flops 10000000 | bytes 4000000 | tf_op jit(solution)/shard_map/tables/pallas_call | solution.py:223
  15.2 12.2 %all-to-all-done.kv_ref = bf16[16,128,256]{2,1,0:T(8,128)(2,1)S(1)} async-done(((bf16[16,128,256]{2,1,0:T(8,128)(2,1)}), bf16[16,128,256]{2,1,0:T(8,128)(2,1)S(1)}, u32[]{:S(2)}, u32[]{:S(2)}) %all-to-all-start) | async-done | bytes 1048608 | tf_op jit(solution)/shard_map/all_to_all | solution.py:222
  27.4 6.0 %attention.1 = (bf16[16,128,256]{2,1,0:T(8,128)(2,1)S(1)}, bf16[128,768]{1,0:T(8,128)(2,1)}, bf16[128,768]{1,0:T(8,128)(2,1)}) custom-call(s32[8]{0:T(128)S(1)} %get-tuple-element.16.starts_ref, s32[32]{0:T(128)S(1)} %copy-done.4, bf16[16,128,256]{2,1,0:T(8,128)(2,1)S(1)} %all-to-all-done.kv_ref, f32[2048,128]{1,0:T(8,128)S(1)} %get-tuple-element.17.table_ref, ...), custom_call_target="tpu_custom_call" | custom-call | tf_op jit(solution)/shard_map/attention/pallas_call | solution.py:240
  33.4 18.7 %all_to_all.10.parts_ref = bf16[16,128,256]{2,1,0:T(8,128)(2,1)S(1)} all-to-all(bf16[16,128,256]{2,1,0:T(8,128)(2,1)S(1)} %get-tuple-element.25), channel_id=1, replica_groups=mesh['seq'=32,'cp'=16] {'cp'}, dimensions={0} | all-to-all | bytes 2097152 | tf_op jit(solution)/shard_map/all_to_all | solution.py:263
  52.1 0.8 %sums.1 = (bf16[128,128]{1,0:T(8,128)(2,1)}, bf16[128,128]{1,0:T(8,128)(2,1)}) custom-call(bf16[16,128,256]{2,1,0:T(8,128)(2,1)S(1)} %all_to_all.10.parts_ref, f32[128,128]{1,0:T(8,128)S(1)} %get-tuple-element.18.mine_ref), custom_call_target="tpu_custom_call" | custom-call | tf_op jit(solution)/shard_map/sums/pallas_call | solution.py:264
Async XLA Ops:
  2.5 7.2 %copy-start = (bf16[128,768]{1,0:T(8,128)(2,1)S(1)}, bf16[128,768]{1,0:T(8,128)(2,1)}, u32[]{:S(2)}) copy-start(bf16[128,768]{1,0:T(8,128)(2,1)} %queries_ref.1) | copy-start | bytes 589828
  2.5 7.2 %copy-start.1 = (bf16[128,768]{1,0:T(8,128)(2,1)S(1)}, bf16[128,768]{1,0:T(8,128)(2,1)}, u32[]{:S(2)}) copy-start(bf16[128,768]{1,0:T(8,128)(2,1)} %grad_ref.1) | copy-start | bytes 589828
  2.5 7.2 %copy-start.2 = (s32[3,2048]{1,0:T(4,128)S(1)}, s32[3,2048]{1,0:T(4,128)}, u32[]{:S(2)}) copy-start(s32[3,2048]{1,0:T(4,128)} %pos_ref.1) | copy-start | bytes 73732
  2.5 7.2 %copy-start.3 = (s32[2048]{0:T(1024)S(1)}, s32[2048]{0:T(1024)}, u32[]{:S(2)}) copy-start(s32[2048]{0:T(1024)} %param.12) | copy-start | bytes 24580
  2.5 24.9 %all-to-all-start = ((bf16[16,128,256]{2,1,0:T(8,128)(2,1)}), bf16[16,128,256]{2,1,0:T(8,128)(2,1)S(1)}, u32[]{:S(2)}, u32[]{:S(2)}) async-start(bf16[16,128,256]{2,1,0:T(8,128)(2,1)} %broadcast_in_dim.3), calls=%async_computation | async-start | bytes 2097152 | tf_op jit(solution)/shard_map/all_to_all | solution.py:222
  9.7 0.7 %copy-start.4 = (s32[32]{0:T(128)S(1)}, s32[32]{0:T(128)}, u32[]{:S(2)}) copy-start(s32[32]{0:T(128)} %order_ref.3) | copy-start | bytes 388

commit v3 on v2

--- a/solution.py
+++ b/solution.py
@@ -44,44 +44,48 @@
     return x * cosine - pltpu.roll(x, HALF, 1) * signed_sine
 
 
-def expanded(table):
-    column = lax.broadcasted_iota(jnp.int32, (1, HD), 1)
-    other = pltpu.roll(table, HALF, 1)
-    return jnp.where(column < HALF, table, other), jnp.where(column < HALF, -other, table)
-
-
-def tables_kernel(
-    order_ref, pos_ref, docs_ref, queries_ref, grad_ref,
-    table_ref, mine_ref, q_ref, do_ref, q_t_ref, do_t_ref, starts_ref,
+def prepare_kernel(
+    order_ref, keys_ref, values_ref, pos_ref, docs_ref, queries_ref, grad_ref,
+    payload_ref, cos_ref, sin_ref, q_ref, do_ref, q_t_ref, do_t_ref, starts_ref,
 ):
     me = lax.axis_index("cp")
+    rows = keys_ref.shape[0]
+    lane = lax.broadcasted_iota(jnp.int32, (1, rows), 1)
+    windows = []
+    for place in range(2):
+        stretch = order_ref[2 * me + place]
+        start = pl.multiple_of((stretch // 2) * 128, 128)
+        window = pos_ref[:, pl.ds(start, 128)].astype(F32)
+        turned = pltpu.roll(window, HALF, 1)
+        windows.append(jnp.where(stretch % 2 == place, window, turned))
+    pos = jnp.where(lane < STRETCH, windows[0], windows[1])
     pair = lax.broadcasted_iota(jnp.int32, (HALF, 1), 0)
     freq = jnp.exp(-(2.0 * pair.astype(F32) / HD) * math.log(1000000.0))
-
-    def some_tokens(c, carry):
-        at = pl.ds(pl.multiple_of(c * 128, 128), 128)
-        pos = pos_ref[:, at].astype(F32)
-        chosen = jnp.where(
-            pair < SEC_T, pos[0:1, :], jnp.where(pair < SEC_T + SEC_H, pos[1:2, :], pos[2:3, :])
-        )
-        angle = chosen * freq
-        table_ref[at, :] = jnp.concatenate([jnp.cos(angle), jnp.sin(angle)], axis=0).T
-        return carry
-
-    lax.fori_loop(0, pos_ref.shape[1] // 128, some_tokens, 0)
+    chosen = jnp.where(
+        pair < SEC_T, pos[0:1, :], jnp.where(pair < SEC_T + SEC_H, pos[1:2, :], pos[2:3, :])
+    )
+    angle = chosen * freq
+    table = jnp.concatenate([jnp.cos(angle), jnp.sin(angle)], axis=0).T
+    other = pltpu.roll(table, HALF, 1)
+    column = lax.broadcasted_iota(jnp.int32, (1, HD), 1)
+    cosine = jnp.where(column < HALF, table, other)
+    signed_sine = jnp.where(column < HALF, -other, table)
+    cos_ref[...] = cosine
+    sin_ref[...] = signed_sine
+    k_rot = rotated(keys_ref[...].astype(F32), cosine, signed_sine).astype(BF16)
+    values = values_ref[...]
+    for peer in range(payload_ref.shape[0]):
+        payload_ref[peer, :, :HD] = k_rot
+        payload_ref[peer, :, HD:] = values
     for place in range(2):
-        rows = pl.ds(place * STRETCH, STRETCH)
-        first = pl.multiple_of(order_ref[2 * me + place] * STRETCH, STRETCH)
-        table = table_ref[pl.ds(first, STRETCH), :]
-        mine_ref[rows, :] = table
-        cosine, signed_sine = expanded(table)
+        part = slice(place * STRETCH, (place + 1) * STRETCH)
         for head in range(HQ):
-            cols = pl.ds(head * HD, HD)
+            cols = slice(head * HD, (head + 1) * HD)
             to = pl.ds(place * LANES + head * STRETCH, STRETCH)
             q_ref[to, :] = rotated(
-                queries_ref[rows, cols].astype(F32), cosine, signed_sine
+                queries_ref[part, cols].astype(F32), cosine[part], signed_sine[part]
             ).astype(BF16)
-            do_ref[to, :] = grad_ref[rows, cols]
+            do_ref[to, :] = grad_ref[part, cols]
         half = pl.ds(place * LANES, LANES)
         q_t_ref[place] = q_ref[half, :].T
         do_t_ref[place] = do_ref[half, :].T
@@ -91,7 +95,7 @@
 
 
 def attention_kernel(
-    starts_ref, order_ref, kv_ref, table_ref, mine_ref, q_ref, do_ref, q_t_ref, do_t_ref,
+    starts_ref, order_ref, kv_ref, cos_ref, sin_ref, q_ref, do_ref, q_t_ref, do_t_ref,
     part_ref, out_ref, dq_ref,
     k_seq, v_seq, e_buf, dp_buf, dk_acc, dv_acc, out_buf, dq_buf, sems,
 ):
@@ -100,9 +104,7 @@
     for block in range(blocks):
         to = pl.ds(pl.multiple_of(order_ref[block] * STRETCH, STRETCH), STRETCH)
         rows = pl.ds((block % 2) * STRETCH, STRETCH)
-        k_seq[to, :] = rotated(
-            kv_ref[block // 2, rows, :HD].astype(F32), *expanded(table_ref[to, :])
-        ).astype(BF16)
+        k_seq[to, :] = kv_ref[block // 2, rows, :HD]
         v_seq[to, :] = kv_ref[block // 2, rows, HD:]
     dk_acc[...] = jnp.zeros_like(dk_acc)
     dv_acc[...] = jnp.zeros_like(dv_acc)
@@ -162,12 +164,10 @@
             ds_cols.append(jnp.concatenate(ds_rows, axis=0))
         p = jnp.concatenate(p_cols, axis=1)
         ds = jnp.concatenate(ds_cols, axis=1)
-        dv_acc[window, :] += dot_nn(p, do_ref[mine, :])
-        dk_acc[window, :] += dot_nn(ds, q_ref[mine, :])
         out = dot_tn(v_seq[window, :], p).T
         dq = dot_tn(k_seq[window, :], ds).T * SCALE
         rows = pl.ds(pl.multiple_of(place * STRETCH, STRETCH), STRETCH)
-        cosine, signed_sine = expanded(mine_ref[rows, :])
+        cosine, signed_sine = cos_ref[rows, :], sin_ref[rows, :]
         for head in range(HQ):
             cols = slice(head * HD, (head + 1) * HD)
             part = slice(head * STRETCH, (head + 1) * STRETCH)
@@ -175,6 +175,8 @@
             dq_buf[rows, cols] = rotated_back(dq[part], cosine, signed_sine).astype(BF16)
         for copy in results(place):
             copy.start()
+        dv_acc[window, :] += dot_nn(p, do_ref[mine, :])
+        dk_acc[window, :] += dot_nn(ds, q_ref[mine, :])
         return carry
 
     def results(place):
@@ -195,12 +197,16 @@
             copy.wait()
 
 
-def sums_kernel(parts_ref, mine_ref, dk_ref, dv_ref):
+def sums_kernel(parts_ref, cos_ref, sin_ref, dk_ref, dv_ref):
     total = parts_ref[0].astype(F32)
     for peer in range(1, parts_ref.shape[0]):
         total = total + parts_ref[peer].astype(F32)
-    dk_ref[...] = rotated_back(total[:, :HD], *expanded(mine_ref[...])).astype(BF16)
+    dk_ref[...] = rotated_back(total[:, :HD], cos_ref[...], sin_ref[...]).astype(BF16)
     dv_ref[...] = total[:, HD:].astype(BF16)
+
+
+def in_hbm(x):
+    return pltpu.with_memory_space_constraint(x, pltpu.HBM)
 
 
 def params(mib):
@@ -217,13 +223,13 @@
     rows = queries.shape[0]
     total = rows * devices
     shape = jax.ShapeDtypeStruct
-    both = jnp.concatenate([keys, values], axis=1)
-    payload = jnp.broadcast_to(both, (devices, *both.shape))
-    kv = lax.all_to_all(payload, "cp", 0, 0, tiled=True)
-    table, mine, q_rows, do_rows, q_cols, do_cols, starts = pl.pallas_call(
-        tables_kernel,
+    stretch_order = in_hbm(stretch_order)
+    docs = doc_ids.reshape(total // 128, 128)
+    payload, cosine, sine, q_rows, do_rows, q_cols, do_cols, starts = pl.pallas_call(
+        prepare_kernel,
         out_shape=(
-            shape((total, HD), F32),
+            shape((devices, rows, 2 * HD), BF16),
+            shape((rows, HD), F32),
             shape((rows, HD), F32),
             shape((2 * LANES, HD), BF16),
             shape((2 * LANES, HD), BF16),
@@ -231,12 +237,15 @@
             shape((2, HD, LANES), BF16),
             shape((DOCS,), jnp.int32),
         ),
-        in_specs=[SMEM, VMEM, VMEM, VMEM, VMEM],
-        out_specs=(VMEM,) * 6 + (SMEM,),
+        in_specs=[SMEM] + [VMEM] * 6,
+        out_specs=(VMEM,) * 7 + (SMEM,),
         compiler_params=params(16),
-        name="tables",
-        cost_estimate=pl.CostEstimate(flops=10**7, transcendentals=0, bytes_accessed=4 * 10**6),
-    )(stretch_order, positions, doc_ids.reshape(total // 128, 128), queries, out_grad)
+        name="prepare",
+    )(
+        stretch_order,
+        *(in_hbm(x) for x in (keys, values, positions, docs, queries, out_grad)),
+    )
+    kv = lax.all_to_all(payload, "cp", 0, 0, tiled=True)
     part, attn_out, grad_queries = pl.pallas_call(
         attention_kernel,
         out_shape=(
@@ -259,16 +268,16 @@
         ],
         compiler_params=params(24),
         name="attention",
-    )(starts, stretch_order, kv, table, mine, q_rows, do_rows, q_cols, do_cols)
+    )(starts, stretch_order, kv, cosine, sine, q_rows, do_rows, q_cols, do_cols)
     parts = lax.all_to_all(part, "cp", 0, 0, tiled=True)
     grad_keys, grad_values = pl.pallas_call(
         sums_kernel,
         out_shape=(shape((rows, HD), BF16), shape((rows, HD), BF16)),
-        in_specs=[VMEM] * 2,
+        in_specs=[VMEM] * 3,
         out_specs=(VMEM, VMEM),
         compiler_params=params(16),
         name="sums",
-    )(parts, mine)
+    )(parts, cosine, sine)
     return attn_out, grad_queries, grad_keys, grad_values
 
 

time: 53.2 us -> 52.6 us (0.989)
  blocking collectives: 18.7 us -> 43.2 us
  waiting for transfers between devices: 12.2 us -> 0 us
  starting transfers between devices: 7.18 us -> 0 us
  Pallas kernels: 11.7 us -> 8.47 us
  local copies, waits for them, and re-layouts: 1.69 us -> 0 us
  other arithmetic: 0.78 us -> 0 us
    all_to_all x0 -> x1, blocking collectives: none -> 23.7 us  [shards(): kv = lax.all_to_all(payload, 'cp', 0, 0, tiled=True)]
    all_to_all x1 -> x0, waiting for transfers between devices: 12.2 us -> none  [shards(): kv = lax.all_to_all(payload, 'cp', 0, 0, tiled=True)]
    all_to_all x1 -> x0, starting transfers between devices: 7.18 us -> none  [shards(): kv = lax.all_to_all(payload, 'cp', 0, 0, tiled=True)]
    pallas_call x1, Pallas kernels: 4.82 us -> 2.06 us  [shards(): pl.pallas_call(prepare_kernel, out_shape=(shape((devices, rows, 2 * HD),...]
    broadcast_in_dim x1 -> x0, local copies, waits for them, and re-layouts: 1.06 us -> none  [shards(): payload = jnp.broadcast_to(both, (devices, *both.shape))]
    all_to_all x1, blocking collectives: 18.7 us -> 19.6 us  [shards(): parts = lax.all_to_all(part, 'cp', 0, 0, tiled=True)]
    concatenate x1 -> x0, other arithmetic: 0.78 us -> none  [shards(): both = jnp.concatenate([keys, values], axis=1)]
    unnamed x10 -> x0, local copies, waits for them, and re-layouts: 0.63 us -> none
  transfers between devices with their start and end apart: 1 -> 0, of which waited for: 1 -> 0; matrix products, arithmetic and copies ran while one was open for 0% -> 0% of each run, Pallas kernels for 9% -> 0%
where the time goes in v3:
time: 52.6 us; the launch traced here: 52.4 us
  blocking collectives  43.2 us (82%)
  Pallas kernels  8.47 us (16%)
  between operations  0.65 us (1%)
    all_to_all x1, blocking collectives, shards(): kv = lax.all_to_all(payload, 'cp', 0, 0, tiled=True)  23.7 us
    all_to_all x1, blocking collectives, shards(): parts = lax.all_to_all(part, 'cp', 0, 0, tiled=True)  19.6 us
    pallas_call x1, Pallas kernels, shards(): pl.pallas_call(attention_kernel, out_shape=(shape((devices, rows, 2 * HD)...  5.58 us
    pallas_call x1, Pallas kernels, shards(): pl.pallas_call(prepare_kernel, out_shape=(shape((devices, rows, 2 * HD),...  2.06 us

profile of v3, /device:TPU:480, one launch (start us, length us, event | category | flops | bytes accessed | tf_op | source)
XLA Modules:
  0.0 52.4 jit_solution(4259111571083382187)
XLA Ops:
  0.6 2.1 %prepare.1 = (bf16[16,128,256]{2,1,0:T(8,128)(2,1)S(1)}, f32[128,128]{1,0:T(8,128)S(1)}, f32[128,128]{1,0:T(8,128)S(1)}, bf16[768,128]{1,0:T(8,128)(2,1)S(1)}, b...) custom-call(s32[32]{0:T(128)} %order_ref.3, ...), custom_call_target="tpu_custom_call" | custom-call | tf_op jit(solution)/shard_map/prepare/pallas_call | solution.py:228
  2.7 23.7 %all_to_all.10.kv_ref = bf16[16,128,256]{2,1,0:T(8,128)(2,1)S(1)} all-to-all(bf16[16,128,256]{2,1,0:T(8,128)(2,1)S(1)} %get-tuple-element.18), channel_id=1, replica_groups=mesh['seq'=32,'cp'=16] {'cp'}, dimensions={0} | all-to-all | bytes 2097152 | tf_op jit(solution)/shard_map/all_to_all | solution.py:248
  26.4 5.6 %attention.1 = (bf16[16,128,256]{2,1,0:T(8,128)(2,1)S(1)}, bf16[128,768]{1,0:T(8,128)(2,1)}, bf16[128,768]{1,0:T(8,128)(2,1)}) custom-call(s32[8]{0:T(128)S(1)} %get-tuple-element.17.starts_ref, s32[32]{0:T(128)} %order_ref.3, bf16[16,128,256]{2,1,0:T(8,128)(2,1)S(1)} %all_to_all.10.kv_ref, f32[128,128]{1,0:T(8,128)S(1)} %get-tuple-element.19.cos_ref, ...), custom_call_target="tpu_custom_call" | custom-call | tf_op jit(solution)/shard_map/attention/pallas_call | solution.py:249
  32.0 19.6 %all_to_all.11.parts_ref = bf16[16,128,256]{2,1,0:T(8,128)(2,1)S(1)} all-to-all(bf16[16,128,256]{2,1,0:T(8,128)(2,1)S(1)} %get-tuple-element.27), channel_id=1, replica_groups=mesh['seq'=32,'cp'=16] {'cp'}, dimensions={0} | all-to-all | bytes 2097152 | tf_op jit(solution)/shard_map/all_to_all | solution.py:272
  51.5 0.8 %sums.1 = (bf16[128,128]{1,0:T(8,128)(2,1)}, bf16[128,128]{1,0:T(8,128)(2,1)}) custom-call(bf16[16,128,256]{2,1,0:T(8,128)(2,1)S(1)} %all_to_all.11.parts_ref, f32[128,128]{1,0:T(8,128)S(1)} %get-tuple-element.19.cos_ref, f32[128,128]{1,0:T(8,128)S(1)} %get-tuple-element.20.sin_ref), custom_call_target="tpu_custom_call" | custom-call | tf_op jit(solution)/shard_map/sums/pallas_call | solution.py:273

commit v4 on v3

--- a/solution.py
+++ b/solution.py
@@ -46,7 +46,7 @@
 
 def prepare_kernel(
     order_ref, keys_ref, values_ref, pos_ref, docs_ref, queries_ref, grad_ref,
-    payload_ref, cos_ref, sin_ref, q_ref, do_ref, q_t_ref, do_t_ref, starts_ref,
+    payload_ref, cos_ref, sin_ref, q_ref, do_ref, q_t_ref, do_t_ref, facts_ref,
 ):
     me = lax.axis_index("cp")
     rows = keys_ref.shape[0]
@@ -90,19 +90,31 @@
         q_t_ref[place] = q_ref[half, :].T
         do_t_ref[place] = do_ref[half, :].T
     docs = docs_ref[...]
-    for doc in range(DOCS):
-        starts_ref[doc] = jnp.sum((docs < doc).astype(jnp.int32))
+    starts = [jnp.sum((docs < doc).astype(jnp.int32)) for doc in range(DOCS)]
+    lanes = lax.broadcasted_iota(jnp.int32, (1, 128), 1)
+    order = jnp.zeros((1, 128), jnp.int32)
+    for block in range(order_ref.shape[0]):
+        order = jnp.where(lanes == block, order_ref[block], order)
+    firsts = [order_ref[2 * me + place] * STRETCH for place in range(2)]
+    facts_ref[0:1, :] = order
+    facts_ref[1:2, :] = jnp.where(lanes == 0, firsts[0], firsts[1])
+    for place, first in enumerate(firsts):
+        token = first + lanes % STRETCH
+        low = jnp.zeros((1, 128), jnp.int32)
+        for start in starts:
+            low = jnp.where(start <= token, jnp.maximum(low, start), low)
+        facts_ref[2 + place : 3 + place, :] = low
+        facts_ref[4 + place : 5 + place, :] = token
 
 
 def attention_kernel(
-    starts_ref, order_ref, kv_ref, cos_ref, sin_ref, q_ref, do_ref, q_t_ref, do_t_ref,
+    facts_ref, kv_ref, cos_ref, sin_ref, q_ref, do_ref, q_t_ref, do_t_ref,
     part_ref, out_ref, dq_ref,
     k_seq, v_seq, e_buf, dp_buf, dk_acc, dv_acc, out_buf, dq_buf, sems,
 ):
-    me = lax.axis_index("cp")
     blocks = k_seq.shape[0] // STRETCH
     for block in range(blocks):
-        to = pl.ds(pl.multiple_of(order_ref[block] * STRETCH, STRETCH), STRETCH)
+        to = pl.ds(pl.multiple_of(facts_ref[0, block] * STRETCH, STRETCH), STRETCH)
         rows = pl.ds((block % 2) * STRETCH, STRETCH)
         k_seq[to, :] = kv_ref[block // 2, rows, :HD]
         v_seq[to, :] = kv_ref[block // 2, rows, HD:]
@@ -110,7 +122,6 @@
     dv_acc[...] = jnp.zeros_like(dv_acc)
     tiles = [slice(j * 128, (j + 1) * 128) for j in range(LANES // 128)]
     steps = range(0, WINDOW, SUB)
-    lane = lax.broadcasted_iota(jnp.int32, (1, 128), 1)
     down = lax.broadcasted_iota(jnp.int32, (SUB, 128), 0)
     factor = SCALE * LOG2E
 
@@ -118,12 +129,9 @@
         return how(x.reshape(SUB // 8, 8, 128), axis=0)
 
     def one_stretch(place, carry):
-        first = order_ref[2 * me + place] * STRETCH
-        token = first + lane % STRETCH
-        low = jnp.zeros_like(token)
-        for doc in range(DOCS):
-            start = starts_ref[doc]
-            low = jnp.where(start <= token, jnp.maximum(low, start), low)
+        first = jnp.where(place == 0, facts_ref[1, 0], facts_ref[1, 1])
+        low = facts_ref[pl.ds(2 + place, 1), :]
+        token = facts_ref[pl.ds(4 + place, 1), :]
         base = pl.multiple_of(jnp.maximum(first + STRETCH - WINDOW, 0), STRETCH)
         window = pl.ds(base, WINDOW)
         mine = pl.ds(pl.multiple_of(place * LANES, LANES), LANES)
@@ -188,7 +196,7 @@
 
     lax.fori_loop(0, 2, one_stretch, 0)
     for block in range(blocks):
-        at = pl.ds(pl.multiple_of(order_ref[block] * STRETCH, STRETCH), STRETCH)
+        at = pl.ds(pl.multiple_of(facts_ref[0, block] * STRETCH, STRETCH), STRETCH)
         rows = pl.ds((block % 2) * STRETCH, STRETCH)
         part_ref[block // 2, rows, :HD] = (dk_acc[at, :] * SCALE).astype(BF16)
         part_ref[block // 2, rows, HD:] = dv_acc[at, :].astype(BF16)
@@ -223,9 +231,8 @@
     rows = queries.shape[0]
     total = rows * devices
     shape = jax.ShapeDtypeStruct
-    stretch_order = in_hbm(stretch_order)
     docs = doc_ids.reshape(total // 128, 128)
-    payload, cosine, sine, q_rows, do_rows, q_cols, do_cols, starts = pl.pallas_call(
+    payload, cosine, sine, q_rows, do_rows, q_cols, do_cols, facts = pl.pallas_call(
         prepare_kernel,
         out_shape=(
             shape((devices, rows, 2 * HD), BF16),
@@ -235,15 +242,14 @@
             shape((2 * LANES, HD), BF16),
             shape((2, HD, LANES), BF16),
             shape((2, HD, LANES), BF16),
-            shape((DOCS,), jnp.int32),
+            shape((8, 128), jnp.int32),
         ),
         in_specs=[SMEM] + [VMEM] * 6,
-        out_specs=(VMEM,) * 7 + (SMEM,),
+        out_specs=(VMEM,) * 8,
         compiler_params=params(16),
         name="prepare",
     )(
-        stretch_order,
-        *(in_hbm(x) for x in (keys, values, positions, docs, queries, out_grad)),
+        *(in_hbm(x) for x in (stretch_order, keys, values, positions, docs, queries, out_grad)),
     )
     kv = lax.all_to_all(payload, "cp", 0, 0, tiled=True)
     part, attn_out, grad_queries = pl.pallas_call(
@@ -253,7 +259,7 @@
             shape((rows, HQ * HD), BF16),
             shape((rows, HQ * HD), BF16),
         ),
-        in_specs=[SMEM, SMEM] + [VMEM] * 7,
+        in_specs=[VMEM] * 8,
         out_specs=(VMEM, HBM, HBM),
         scratch_shapes=[
             pltpu.VMEM((total, HD), BF16),
@@ -268,7 +274,7 @@
         ],
         compiler_params=params(24),
         name="attention",
-    )(starts, stretch_order, kv, cosine, sine, q_rows, do_rows, q_cols, do_cols)
+    )(facts, kv, cosine, sine, q_rows, do_rows, q_cols, do_cols)
     parts = lax.all_to_all(part, "cp", 0, 0, tiled=True)
     grad_keys, grad_values = pl.pallas_call(
         sums_kernel,

time: 52.6 us -> 51.8 us (0.985)
  Pallas kernels: 8.47 us -> 7.76 us
where the time goes in v4:
time: 51.8 us; the launch traced here: 51.6 us
  blocking collectives  43.2 us (83%)
  Pallas kernels  7.76 us (15%)
  between operations  0.65 us (1%)
    all_to_all x1, blocking collectives, shards(): kv = lax.all_to_all(payload, 'cp', 0, 0, tiled=True)  23.7 us
    all_to_all x1, blocking collectives, shards(): parts = lax.all_to_all(part, 'cp', 0, 0, tiled=True)  19.6 us
    pallas_call x1, Pallas kernels, shards(): pl.pallas_call(attention_kernel, out_shape=(shape((devices, rows, 2 * HD)...  5.12 us
    pallas_call x1, Pallas kernels, shards(): pl.pallas_call(prepare_kernel, out_shape=(shape((devices, rows, 2 * HD),...  1.81 us

profile of v4, /device:TPU:480, one launch (start us, length us, event | category | flops | bytes accessed | tf_op | source)
XLA Modules:
  0.0 51.6 jit_solution(12169880347679034122)
XLA Ops:
  0.6 1.8 %prepare.1 = (bf16[16,128,256]{2,1,0:T(8,128)(2,1)S(1)}, f32[128,128]{1,0:T(8,128)S(1)}, f32[128,128]{1,0:T(8,128)S(1)}, bf16[768,128]{1,0:T(8,128)(2,1)S(1)}, b...) custom-call(s32[32]{0:T(128)} %order_ref.1, ...), custom_call_target="tpu_custom_call" | custom-call | tf_op jit(solution)/shard_map/prepare/pallas_call | solution.py:235
  2.4 23.7 %all_to_all.10.kv_ref = bf16[16,128,256]{2,1,0:T(8,128)(2,1)S(1)} all-to-all(bf16[16,128,256]{2,1,0:T(8,128)(2,1)S(1)} %get-tuple-element.18), channel_id=1, replica_groups=mesh['seq'=32,'cp'=16] {'cp'}, dimensions={0} | all-to-all | bytes 2097152 | tf_op jit(solution)/shard_map/all_to_all | solution.py:254
  26.1 5.1 %attention.1 = (bf16[16,128,256]{2,1,0:T(8,128)(2,1)S(1)}, bf16[128,768]{1,0:T(8,128)(2,1)}, bf16[128,768]{1,0:T(8,128)(2,1)}) custom-call(s32[8,128]{1,0:T(8,128)S(1)} %get-tuple-element.17.facts_ref, bf16[16,128,256]{2,1,0:T(8,128)(2,1)S(1)} %all_to_all.10.kv_ref, f32[128,128]{1,0:T(8,128)S(1)} %get-tuple-element.19.cos_ref, ...), custom_call_target="tpu_custom_call" | custom-call | tf_op jit(solution)/shard_map/attention/pallas_call | solution.py:255
  31.3 19.6 %all_to_all.11.parts_ref = bf16[16,128,256]{2,1,0:T(8,128)(2,1)S(1)} all-to-all(bf16[16,128,256]{2,1,0:T(8,128)(2,1)S(1)} %get-tuple-element.27), channel_id=1, replica_groups=mesh['seq'=32,'cp'=16] {'cp'}, dimensions={0} | all-to-all | bytes 2097152 | tf_op jit(solution)/shard_map/all_to_all | solution.py:278
  50.8 0.8 %sums.1 = (bf16[128,128]{1,0:T(8,128)(2,1)}, bf16[128,128]{1,0:T(8,128)(2,1)}) custom-call(bf16[16,128,256]{2,1,0:T(8,128)(2,1)S(1)} %all_to_all.11.parts_ref, f32[128,128]{1,0:T(8,128)S(1)} %get-tuple-element.19.cos_ref, f32[128,128]{1,0:T(8,128)S(1)} %get-tuple-element.20.sin_ref), custom_call_target="tpu_custom_call" | custom-call | tf_op jit(solution)/shard_map/sums/pallas_call | solution.py:279

commit v5 on v4

--- a/solution.py
+++ b/solution.py
@@ -45,8 +45,7 @@
 
 
 def prepare_kernel(
-    order_ref, keys_ref, values_ref, pos_ref, docs_ref, queries_ref, grad_ref,
-    payload_ref, cos_ref, sin_ref, q_ref, do_ref, q_t_ref, do_t_ref, facts_ref,
+    order_ref, keys_ref, values_ref, pos_ref, docs_ref, payload_ref, cos_ref, sin_ref, facts_ref
 ):
     me = lax.axis_index("cp")
     rows = keys_ref.shape[0]
@@ -77,18 +76,6 @@
     for peer in range(payload_ref.shape[0]):
         payload_ref[peer, :, :HD] = k_rot
         payload_ref[peer, :, HD:] = values
-    for place in range(2):
-        part = slice(place * STRETCH, (place + 1) * STRETCH)
-        for head in range(HQ):
-            cols = slice(head * HD, (head + 1) * HD)
-            to = pl.ds(place * LANES + head * STRETCH, STRETCH)
-            q_ref[to, :] = rotated(
-                queries_ref[part, cols].astype(F32), cosine[part], signed_sine[part]
-            ).astype(BF16)
-            do_ref[to, :] = grad_ref[part, cols]
-        half = pl.ds(place * LANES, LANES)
-        q_t_ref[place] = q_ref[half, :].T
-        do_t_ref[place] = do_ref[half, :].T
     docs = docs_ref[...]
     starts = [jnp.sum((docs < doc).astype(jnp.int32)) for doc in range(DOCS)]
     lanes = lax.broadcasted_iota(jnp.int32, (1, 128), 1)
@@ -108,10 +95,23 @@
 
 
 def attention_kernel(
-    facts_ref, kv_ref, cos_ref, sin_ref, q_ref, do_ref, q_t_ref, do_t_ref,
+    facts_ref, kv_ref, cos_ref, sin_ref, queries_ref, grad_ref,
     part_ref, out_ref, dq_ref,
-    k_seq, v_seq, e_buf, dp_buf, dk_acc, dv_acc, out_buf, dq_buf, sems,
+    q_ref, do_ref, q_t_ref, do_t_ref, k_seq, v_seq, e_buf, dp_buf, dk_acc, dv_acc, out_buf, dq_buf, sems,
 ):
+    cosine, signed_sine = cos_ref[...], sin_ref[...]
+    for place in range(2):
+        part = slice(place * STRETCH, (place + 1) * STRETCH)
+        for head in range(HQ):
+            cols = slice(head * HD, (head + 1) * HD)
+            to = pl.ds(place * LANES + head * STRETCH, STRETCH)
+            q_ref[to, :] = rotated(
+                queries_ref[part, cols].astype(F32), cosine[part], signed_sine[part]
+            ).astype(BF16)
+            do_ref[to, :] = grad_ref[part, cols]
+        half = pl.ds(place * LANES, LANES)
+        q_t_ref[place] = q_ref[half, :].T
+        do_t_ref[place] = do_ref[half, :].T
     blocks = k_seq.shape[0] // STRETCH
     for block in range(blocks):
         to = pl.ds(pl.multiple_of(facts_ref[0, block] * STRETCH, STRETCH), STRETCH)
@@ -232,24 +232,20 @@
     total = rows * devices
     shape = jax.ShapeDtypeStruct
     docs = doc_ids.reshape(total // 128, 128)
-    payload, cosine, sine, q_rows, do_rows, q_cols, do_cols, facts = pl.pallas_call(
+    payload, cosine, sine, facts = pl.pallas_call(
         prepare_kernel,
         out_shape=(
             shape((devices, rows, 2 * HD), BF16),
             shape((rows, HD), F32),
             shape((rows, HD), F32),
-            shape((2 * LANES, HD), BF16),
-            shape((2 * LANES, HD), BF16),
-            shape((2, HD, LANES), BF16),
-            shape((2, HD, LANES), BF16),
             shape((8, 128), jnp.int32),
         ),
-        in_specs=[SMEM] + [VMEM] * 6,
-        out_specs=(VMEM,) * 8,
+        in_specs=[SMEM] + [VMEM] * 4,
+        out_specs=(VMEM,) * 4,
         compiler_params=params(16),
         name="prepare",
     )(
-        *(in_hbm(x) for x in (stretch_order, keys, values, positions, docs, queries, out_grad)),
+        *(in_hbm(x) for x in (stretch_order, keys, values, positions, docs)),
     )
     kv = lax.all_to_all(payload, "cp", 0, 0, tiled=True)
     part, attn_out, grad_queries = pl.pallas_call(
@@ -259,9 +255,13 @@
             shape((rows, HQ * HD), BF16),
             shape((rows, HQ * HD), BF16),
         ),
-        in_specs=[VMEM] * 8,
+        in_specs=[VMEM] * 6,
         out_specs=(VMEM, HBM, HBM),
         scratch_shapes=[
+            pltpu.VMEM((2 * LANES, HD), BF16),
+            pltpu.VMEM((2 * LANES, HD), BF16),
+            pltpu.VMEM((2, HD, LANES), BF16),
+            pltpu.VMEM((2, HD, LANES), BF16),
             pltpu.VMEM((total, HD), BF16),
             pltpu.VMEM((total, HD), BF16),
             pltpu.VMEM((WINDOW, LANES), F32),
@@ -274,7 +274,7 @@
         ],
         compiler_params=params(24),
         name="attention",
-    )(facts, kv, cosine, sine, q_rows, do_rows, q_cols, do_cols)
+    )(facts, kv, cosine, sine, queries, out_grad)
     parts = lax.all_to_all(part, "cp", 0, 0, tiled=True)
     grad_keys, grad_values = pl.pallas_call(
         sums_kernel,

time: 51.8 us -> 51.9 us (level)
  no operation moved by 1% of the time
where the time goes in v5:
time: 51.9 us; the launch traced here: 51.6 us
  blocking collectives  43.4 us (84%)
  Pallas kernels  7.57 us (15%)
  between operations  0.67 us (1%)
    all_to_all x1, blocking collectives, shards(): kv = lax.all_to_all(payload, 'cp', 0, 0, tiled=True)  23.8 us
    all_to_all x1, blocking collectives, shards(): parts = lax.all_to_all(part, 'cp', 0, 0, tiled=True)  19.6 us
    pallas_call x1, Pallas kernels, shards(): pl.pallas_call(attention_kernel, out_shape=(shape((devices, rows, 2 * HD)...  5.44 us
    pallas_call x1, Pallas kernels, shards(): pl.pallas_call(prepare_kernel, out_shape=(shape((devices, rows, 2 * HD),...  1.31 us

profile of v5, /device:TPU:480, one launch (start us, length us, event | category | flops | bytes accessed | tf_op | source)
XLA Modules:
  0.0 51.6 jit_solution(160282610292727263)
XLA Ops:
  0.6 1.3 %prepare.1 = (bf16[16,128,256]{2,1,0:T(8,128)(2,1)S(1)}, f32[128,128]{1,0:T(8,128)S(1)}, f32[128,128]{1,0:T(8,128)S(1)}, s32[8,128]{1,0:T(8,128)S(1)}) custom-call(s32[32]{0:T(128)} %order_ref.1, bf16[128,128]{1,0:T(8,128)(2,1)} %keys_ref.1, bf16[128,128]{1,0:T(8,128)(2,1)} %values_ref.1, s32[3,2048]{1,0:T(4,128)} %pos_ref.1, s32[16,128]{1,0:T(8,128)} %bitcast.1), custom_call_target="tpu_custom_call" | custom-call | tf_op jit(solution)/shard_map/prepare/pallas_call | solution.py:235
  2.0 0.0 copy-start
  2.0 0.0 copy-start.1
  2.0 23.8 %all_to_all.10.kv_ref = bf16[16,128,256]{2,1,0:T(8,128)(2,1)S(1)} all-to-all(bf16[16,128,256]{2,1,0:T(8,128)(2,1)S(1)} %get-tuple-element.14), channel_id=1, replica_groups=mesh['seq'=32,'cp'=16] {'cp'}, dimensions={0} | all-to-all | bytes 2097152 | tf_op jit(solution)/shard_map/all_to_all | solution.py:250
  25.8 0.0 copy-done
  25.8 0.0 copy-done.1
  25.8 5.4 %attention.1 = (bf16[16,128,256]{2,1,0:T(8,128)(2,1)S(1)}, bf16[128,768]{1,0:T(8,128)(2,1)}, bf16[128,768]{1,0:T(8,128)(2,1)}) custom-call(s32[8,128]{1,0:T(8,128)S(1)} %get-tuple-element.13.facts_ref, bf16[16,128,256]{2,1,0:T(8,128)(2,1)S(1)} %all_to_all.10.kv_ref, f32[128,128]{1,0:T(8,128)S(1)} %get-tuple-element.15.cos_ref, ...), custom_call_target="tpu_custom_call" | custom-call | tf_op jit(solution)/shard_map/attention/pallas_call | solution.py:251
  31.2 19.6 %all_to_all.11.parts_ref = bf16[16,128,256]{2,1,0:T(8,128)(2,1)S(1)} all-to-all(bf16[16,128,256]{2,1,0:T(8,128)(2,1)S(1)} %get-tuple-element.19), channel_id=1, replica_groups=mesh['seq'=32,'cp'=16] {'cp'}, dimensions={0} | all-to-all | bytes 2097152 | tf_op jit(solution)/shard_map/all_to_all | solution.py:278
  50.8 0.8 %sums.1 = (bf16[128,128]{1,0:T(8,128)(2,1)}, bf16[128,128]{1,0:T(8,128)(2,1)}) custom-call(bf16[16,128,256]{2,1,0:T(8,128)(2,1)S(1)} %all_to_all.11.parts_ref, f32[128,128]{1,0:T(8,128)S(1)} %get-tuple-element.15.cos_ref, f32[128,128]{1,0:T(8,128)S(1)} %get-tuple-element.16.sin_ref), custom_call_target="tpu_custom_call" | custom-call | tf_op jit(solution)/shard_map/sums/pallas_call | solution.py:279
Async XLA Ops:
  2.0 23.8 %copy-start = (bf16[128,768]{1,0:T(8,128)(2,1)S(1)}, bf16[128,768]{1,0:T(8,128)(2,1)}, u32[]{:S(2)}) copy-start(bf16[128,768]{1,0:T(8,128)(2,1)} %queries_ref.1) | copy-start | bytes 589828
  2.0 23.8 %copy-start.1 = (bf16[128,768]{1,0:T(8,128)(2,1)S(1)}, bf16[128,768]{1,0:T(8,128)(2,1)}, u32[]{:S(2)}) copy-start(bf16[128,768]{1,0:T(8,128)(2,1)} %grad_ref.1) | copy-start | bytes 589828

commit v6 on v5

--- a/solution.py
+++ b/solution.py
@@ -19,6 +19,8 @@
 LANES = HQ * STRETCH
 SCALE = 1.0 / math.sqrt(HD)
 LOG2E = math.log2(math.e)
+GATHER_ORDER = tuple(range(15, -1, -1))
+SCATTER_ORDER = tuple(range(15, -1, -1))
 
 F32 = jnp.float32
 BF16 = jnp.bfloat16
@@ -116,8 +118,9 @@
     for block in range(blocks):
         to = pl.ds(pl.multiple_of(facts_ref[0, block] * STRETCH, STRETCH), STRETCH)
         rows = pl.ds((block % 2) * STRETCH, STRETCH)
-        k_seq[to, :] = kv_ref[block // 2, rows, :HD]
-        v_seq[to, :] = kv_ref[block // 2, rows, HD:]
+        peer = GATHER_ORDER.index(block // 2)
+        k_seq[to, :] = kv_ref[peer, rows, :HD]
+        v_seq[to, :] = kv_ref[peer, rows, HD:]
     dk_acc[...] = jnp.zeros_like(dk_acc)
     dv_acc[...] = jnp.zeros_like(dv_acc)
     tiles = [slice(j * 128, (j + 1) * 128) for j in range(LANES // 128)]
@@ -198,8 +201,9 @@
     for block in range(blocks):
         at = pl.ds(pl.multiple_of(facts_ref[0, block] * STRETCH, STRETCH), STRETCH)
         rows = pl.ds((block % 2) * STRETCH, STRETCH)
-        part_ref[block // 2, rows, :HD] = (dk_acc[at, :] * SCALE).astype(BF16)
-        part_ref[block // 2, rows, HD:] = dv_acc[at, :].astype(BF16)
+        peer = SCATTER_ORDER.index(block // 2)
+        part_ref[peer, rows, :HD] = (dk_acc[at, :] * SCALE).astype(BF16)
+        part_ref[peer, rows, HD:] = dv_acc[at, :].astype(BF16)
     for place in range(2):
         for copy in results(place):
             copy.wait()
@@ -224,6 +228,10 @@
 VMEM = pl.BlockSpec(memory_space=pltpu.VMEM)
 HBM = pl.BlockSpec(memory_space=pltpu.HBM)
 SMEM = pl.BlockSpec(memory_space=pltpu.SMEM)
+
+
+def exchanged(blocks, order):
+    return lax.all_to_all(blocks, "cp", 0, 0, axis_index_groups=[list(order)], tiled=True)
 
 
 def shards(queries, keys, values, out_grad, positions, doc_ids, stretch_order):
@@ -247,7 +255,7 @@
     )(
         *(in_hbm(x) for x in (stretch_order, keys, values, positions, docs)),
     )
-    kv = lax.all_to_all(payload, "cp", 0, 0, tiled=True)
+    kv = exchanged(payload, GATHER_ORDER)
     part, attn_out, grad_queries = pl.pallas_call(
         attention_kernel,
         out_shape=(
@@ -275,7 +283,7 @@
         compiler_params=params(24),
         name="attention",
     )(facts, kv, cosine, sine, queries, out_grad)
-    parts = lax.all_to_all(part, "cp", 0, 0, tiled=True)
+    parts = exchanged(part, SCATTER_ORDER)
     grad_keys, grad_values = pl.pallas_call(
         sums_kernel,
         out_shape=(shape((rows, HD), BF16), shape((rows, HD), BF16)),

time: 51.9 us -> 49.3 us (0.950)
  blocking collectives: 43.4 us -> 40.8 us
    all_to_all x2, blocking collectives: 43.4 us -> 40.8 us  [exchanged(): lax.all_to_all(blocks, 'cp', 0, 0, axis_index_groups=[list(order)], tiled...]
where the time goes in v6:
time: 49.3 us; the launch traced here: 49.1 us
  blocking collectives  40.8 us (83%)
  Pallas kernels  7.57 us (15%)
  between operations  0.67 us (1%)
    all_to_all x2, blocking collectives, exchanged(): lax.all_to_all(blocks, 'cp', 0, 0, axis_index_groups=[list(order)], tiled...  40.8 us
    pallas_call x1, Pallas kernels, shards(): pl.pallas_call(attention_kernel, out_shape=(shape((devices, rows, 2 * HD)...  5.43 us
    pallas_call x1, Pallas kernels, shards(): pl.pallas_call(prepare_kernel, out_shape=(shape((devices, rows, 2 * HD),...  1.31 us

profile of v6, /device:TPU:480, one launch (start us, length us, event | category | flops | bytes accessed | tf_op | source)
XLA Modules:
  0.0 49.1 jit_solution(8402069221443478842)
XLA Ops:
  0.6 1.3 %prepare.1 = (bf16[16,128,256]{2,1,0:T(8,128)(2,1)S(1)}, f32[128,128]{1,0:T(8,128)S(1)}, f32[128,128]{1,0:T(8,128)S(1)}, s32[8,128]{1,0:T(8,128)S(1)}) custom-call(s32[32]{0:T(128)} %order_ref.1, bf16[128,128]{1,0:T(8,128)(2,1)} %keys_ref.1, bf16[128,128]{1,0:T(8,128)(2,1)} %values_ref.1, s32[3,2048]{1,0:T(4,128)} %pos_ref.1, s32[16,128]{1,0:T(8,128)} %bitcast.1), custom_call_target="tpu_custom_call" | custom-call | tf_op jit(solution)/shard_map/prepare/pallas_call | solution.py:243
  2.0 0.0 copy-start
  2.0 0.0 copy-start.1
  2.0 21.5 %all_to_all.10.kv_ref = bf16[16,128,256]{2,1,0:T(8,128)(2,1)S(1)} all-to-all(bf16[16,128,256]{2,1,0:T(8,128)(2,1)S(1)} %get-tuple-element.14), channel_id=1, replica_groups={{15,14,13,12,11,10,9,8,7,6,5,4,3,2,1,0},{31,30,29,28,27,26,25,24,23,22,..., dimensions={0} | all-to-all | bytes 2097152 | tf_op jit(solution)/shard_map/all_to_all | solution.py:234
  23.5 0.0 copy-done
  23.5 0.0 copy-done.1
  23.5 5.4 %attention.1 = (bf16[16,128,256]{2,1,0:T(8,128)(2,1)S(1)}, bf16[128,768]{1,0:T(8,128)(2,1)}, bf16[128,768]{1,0:T(8,128)(2,1)}) custom-call(s32[8,128]{1,0:T(8,128)S(1)} %get-tuple-element.13.facts_ref, bf16[16,128,256]{2,1,0:T(8,128)(2,1)S(1)} %all_to_all.10.kv_ref, f32[128,128]{1,0:T(8,128)S(1)} %get-tuple-element.15.cos_ref, ...), custom_call_target="tpu_custom_call" | custom-call | tf_op jit(solution)/shard_map/attention/pallas_call | solution.py:259
  29.0 19.3 %all_to_all.11.parts_ref = bf16[16,128,256]{2,1,0:T(8,128)(2,1)S(1)} all-to-all(bf16[16,128,256]{2,1,0:T(8,128)(2,1)S(1)} %get-tuple-element.19), channel_id=1, replica_groups={{15,14,13,12,11,10,9,8,7,6,5,4,3,2,1,0},{31,30,29,28,27,26,25,24,23,22,..., dimensions={0} | all-to-all | bytes 2097152 | tf_op jit(solution)/shard_map/all_to_all | solution.py:234
  48.3 0.8 %sums.1 = (bf16[128,128]{1,0:T(8,128)(2,1)}, bf16[128,128]{1,0:T(8,128)(2,1)}) custom-call(bf16[16,128,256]{2,1,0:T(8,128)(2,1)S(1)} %all_to_all.11.parts_ref, f32[128,128]{1,0:T(8,128)S(1)} %get-tuple-element.15.cos_ref, f32[128,128]{1,0:T(8,128)S(1)} %get-tuple-element.16.sin_ref), custom_call_target="tpu_custom_call" | custom-call | tf_op jit(solution)/shard_map/sums/pallas_call | solution.py:287
Async XLA Ops:
  2.0 21.6 %copy-start = (bf16[128,768]{1,0:T(8,128)(2,1)S(1)}, bf16[128,768]{1,0:T(8,128)(2,1)}, u32[]{:S(2)}) copy-start(bf16[128,768]{1,0:T(8,128)(2,1)} %queries_ref.1) | copy-start | bytes 589828
  2.0 21.6 %copy-start.1 = (bf16[128,768]{1,0:T(8,128)(2,1)S(1)}, bf16[128,768]{1,0:T(8,128)(2,1)}, u32[]{:S(2)}) copy-start(bf16[128,768]{1,0:T(8,128)(2,1)} %grad_ref.1) | copy-start | bytes 589828

commit v7 on v6

--- a/solution.py
+++ b/solution.py
@@ -19,7 +19,7 @@
 LANES = HQ * STRETCH
 SCALE = 1.0 / math.sqrt(HD)
 LOG2E = math.log2(math.e)
-GATHER_ORDER = tuple(range(15, -1, -1))
+GATHER_ORDER = (11, 15, 9, 1, 12, 2, 14, 10, 0, 4, 7, 6, 13, 5, 3, 8)
 SCATTER_ORDER = tuple(range(15, -1, -1))
 
 F32 = jnp.float32

time: 49.3 us -> 49.3 us (level)
  no operation moved by 1% of the time
where the time goes in v7:
time: 49.3 us; the launch traced here: 49.1 us
  blocking collectives  40.8 us (83%)
  Pallas kernels  7.57 us (15%)
  between operations  0.67 us (1%)
    all_to_all x2, blocking collectives, exchanged(): lax.all_to_all(blocks, 'cp', 0, 0, axis_index_groups=[list(order)], tiled...  40.8 us
    pallas_call x1, Pallas kernels, shards(): pl.pallas_call(attention_kernel, out_shape=(shape((devices, rows, 2 * HD)...  5.44 us
    pallas_call x1, Pallas kernels, shards(): pl.pallas_call(prepare_kernel, out_shape=(shape((devices, rows, 2 * HD),...  1.31 us

profile of v7, /device:TPU:480, one launch (start us, length us, event | category | flops | bytes accessed | tf_op | source)
XLA Modules:
  0.0 49.1 jit_solution(9853314655323938176)
XLA Ops:
  0.6 1.3 %prepare.1 = (bf16[16,128,256]{2,1,0:T(8,128)(2,1)S(1)}, f32[128,128]{1,0:T(8,128)S(1)}, f32[128,128]{1,0:T(8,128)S(1)}, s32[8,128]{1,0:T(8,128)S(1)}) custom-call(s32[32]{0:T(128)} %order_ref.1, bf16[128,128]{1,0:T(8,128)(2,1)} %keys_ref.1, bf16[128,128]{1,0:T(8,128)(2,1)} %values_ref.1, s32[3,2048]{1,0:T(4,128)} %pos_ref.1, s32[16,128]{1,0:T(8,128)} %bitcast.1), custom_call_target="tpu_custom_call" | custom-call | tf_op jit(solution)/shard_map/prepare/pallas_call | solution.py:243
  2.0 0.0 copy-start
  2.0 0.0 copy-start.1
  2.0 21.7 %all_to_all.10.kv_ref = bf16[16,128,256]{2,1,0:T(8,128)(2,1)S(1)} all-to-all(bf16[16,128,256]{2,1,0:T(8,128)(2,1)S(1)} %get-tuple-element.14), channel_id=1, replica_groups={{11,15,9,1,12,2,14,10,0,4,7,6,13,5,3,8},{27,31,25,17,28,18,30,26,16,20,..., dimensions={0} | all-to-all | bytes 2097152 | tf_op jit(solution)/shard_map/all_to_all | solution.py:234
  23.7 0.0 copy-done
  23.7 0.0 copy-done.1
  23.7 5.4 %attention.1 = (bf16[16,128,256]{2,1,0:T(8,128)(2,1)S(1)}, bf16[128,768]{1,0:T(8,128)(2,1)}, bf16[128,768]{1,0:T(8,128)(2,1)}) custom-call(s32[8,128]{1,0:T(8,128)S(1)} %get-tuple-element.13.facts_ref, bf16[16,128,256]{2,1,0:T(8,128)(2,1)S(1)} %all_to_all.10.kv_ref, f32[128,128]{1,0:T(8,128)S(1)} %get-tuple-element.15.cos_ref, ...), custom_call_target="tpu_custom_call" | custom-call | tf_op jit(solution)/shard_map/attention/pallas_call | solution.py:259
  29.1 19.1 %all_to_all.11.parts_ref = bf16[16,128,256]{2,1,0:T(8,128)(2,1)S(1)} all-to-all(bf16[16,128,256]{2,1,0:T(8,128)(2,1)S(1)} %get-tuple-element.19), channel_id=1, replica_groups={{15,14,13,12,11,10,9,8,7,6,5,4,3,2,1,0},{31,30,29,28,27,26,25,24,23,22,..., dimensions={0} | all-to-all | bytes 2097152 | tf_op jit(solution)/shard_map/all_to_all | solution.py:234
  48.2 0.8 %sums.1 = (bf16[128,128]{1,0:T(8,128)(2,1)}, bf16[128,128]{1,0:T(8,128)(2,1)}) custom-call(bf16[16,128,256]{2,1,0:T(8,128)(2,1)S(1)} %all_to_all.11.parts_ref, f32[128,128]{1,0:T(8,128)S(1)} %get-tuple-element.15.cos_ref, f32[128,128]{1,0:T(8,128)S(1)} %get-tuple-element.16.sin_ref), custom_call_target="tpu_custom_call" | custom-call | tf_op jit(solution)/shard_map/sums/pallas_call | solution.py:287
Async XLA Ops:
  2.0 21.7 %copy-start = (bf16[128,768]{1,0:T(8,128)(2,1)S(1)}, bf16[128,768]{1,0:T(8,128)(2,1)}, u32[]{:S(2)}) copy-start(bf16[128,768]{1,0:T(8,128)(2,1)} %queries_ref.1) | copy-start | bytes 589828
  2.0 21.7 %copy-start.1 = (bf16[128,768]{1,0:T(8,128)(2,1)S(1)}, bf16[128,768]{1,0:T(8,128)(2,1)}, u32[]{:S(2)}) copy-start(bf16[128,768]{1,0:T(8,128)(2,1)} %grad_ref.1) | copy-start | bytes 589828

commit v8 on v6

--- a/solution.py
+++ b/solution.py
@@ -197,7 +197,8 @@
             pltpu.make_async_copy(dq_buf.at[rows], dq_ref.at[rows], sems.at[1, place]),
         )
 
-    lax.fori_loop(0, 2, one_stretch, 0)
+    for place in range(2):
+        one_stretch(place, 0)
     for block in range(blocks):
         at = pl.ds(pl.multiple_of(facts_ref[0, block] * STRETCH, STRETCH), STRETCH)
         rows = pl.ds((block % 2) * STRETCH, STRETCH)

time: 49.3 us -> 49.1 us (level)
  no operation moved by 1% of the time
where the time goes in v8:
time: 49.1 us; the launch traced here: 48.9 us
  blocking collectives  40.8 us (83%)
  Pallas kernels  7.35 us (15%)
  between operations  0.67 us (1%)
    all_to_all x2, blocking collectives, exchanged(): lax.all_to_all(blocks, 'cp', 0, 0, axis_index_groups=[list(order)], tiled...  40.8 us
    pallas_call x1, Pallas kernels, shards(): pl.pallas_call(attention_kernel, out_shape=(shape((devices, rows, 2 * HD)...  5.22 us
    pallas_call x1, Pallas kernels, shards(): pl.pallas_call(prepare_kernel, out_shape=(shape((devices, rows, 2 * HD),...  1.31 us

profile of v8, /device:TPU:480, one launch (start us, length us, event | category | flops | bytes accessed | tf_op | source)
XLA Modules:
  0.0 48.9 jit_solution(14197908883768740713)
XLA Ops:
  0.6 1.3 %prepare.1 = (bf16[16,128,256]{2,1,0:T(8,128)(2,1)S(1)}, f32[128,128]{1,0:T(8,128)S(1)}, f32[128,128]{1,0:T(8,128)S(1)}, s32[8,128]{1,0:T(8,128)S(1)}) custom-call(s32[32]{0:T(128)} %order_ref.1, bf16[128,128]{1,0:T(8,128)(2,1)} %keys_ref.1, bf16[128,128]{1,0:T(8,128)(2,1)} %values_ref.1, s32[3,2048]{1,0:T(4,128)} %pos_ref.1, s32[16,128]{1,0:T(8,128)} %bitcast.1), custom_call_target="tpu_custom_call" | custom-call | tf_op jit(solution)/shard_map/prepare/pallas_call | solution.py:244
  2.0 0.0 copy-start
  2.0 0.0 copy-start.1
  2.0 21.5 %all_to_all.10.kv_ref = bf16[16,128,256]{2,1,0:T(8,128)(2,1)S(1)} all-to-all(bf16[16,128,256]{2,1,0:T(8,128)(2,1)S(1)} %get-tuple-element.14), channel_id=1, replica_groups={{15,14,13,12,11,10,9,8,7,6,5,4,3,2,1,0},{31,30,29,28,27,26,25,24,23,22,..., dimensions={0} | all-to-all | bytes 2097152 | tf_op jit(solution)/shard_map/all_to_all | solution.py:235
  23.5 0.0 copy-done
  23.5 0.0 copy-done.1
  23.5 5.2 %attention.1 = (bf16[16,128,256]{2,1,0:T(8,128)(2,1)S(1)}, bf16[128,768]{1,0:T(8,128)(2,1)}, bf16[128,768]{1,0:T(8,128)(2,1)}) custom-call(s32[8,128]{1,0:T(8,128)S(1)} %get-tuple-element.13.facts_ref, bf16[16,128,256]{2,1,0:T(8,128)(2,1)S(1)} %all_to_all.10.kv_ref, f32[128,128]{1,0:T(8,128)S(1)} %get-tuple-element.15.cos_ref, ...), custom_call_target="tpu_custom_call" | custom-call | tf_op jit(solution)/shard_map/attention/pallas_call | solution.py:260
  28.7 19.3 %all_to_all.11.parts_ref = bf16[16,128,256]{2,1,0:T(8,128)(2,1)S(1)} all-to-all(bf16[16,128,256]{2,1,0:T(8,128)(2,1)S(1)} %get-tuple-element.19), channel_id=1, replica_groups={{15,14,13,12,11,10,9,8,7,6,5,4,3,2,1,0},{31,30,29,28,27,26,25,24,23,22,..., dimensions={0} | all-to-all | bytes 2097152 | tf_op jit(solution)/shard_map/all_to_all | solution.py:235
  48.0 0.8 %sums.1 = (bf16[128,128]{1,0:T(8,128)(2,1)}, bf16[128,128]{1,0:T(8,128)(2,1)}) custom-call(bf16[16,128,256]{2,1,0:T(8,128)(2,1)S(1)} %all_to_all.11.parts_ref, f32[128,128]{1,0:T(8,128)S(1)} %get-tuple-element.15.cos_ref, f32[128,128]{1,0:T(8,128)S(1)} %get-tuple-element.16.sin_ref), custom_call_target="tpu_custom_call" | custom-call | tf_op jit(solution)/shard_map/sums/pallas_call | solution.py:288
Async XLA Ops:
  2.0 21.6 %copy-start = (bf16[128,768]{1,0:T(8,128)(2,1)S(1)}, bf16[128,768]{1,0:T(8,128)(2,1)}, u32[]{:S(2)}) copy-start(bf16[128,768]{1,0:T(8,128)(2,1)} %queries_ref.1) | copy-start | bytes 589828
  2.0 21.6 %copy-start.1 = (bf16[128,768]{1,0:T(8,128)(2,1)S(1)}, bf16[128,768]{1,0:T(8,128)(2,1)}, u32[]{:S(2)}) copy-start(bf16[128,768]{1,0:T(8,128)(2,1)} %grad_ref.1) | copy-start | bytes 589828
